TPU v7x, 128 devices: a whole 4x4x4 slice. The times are simulated.
128 devices in a mesh: dp: 4 (over y), tensor: 32 (over z, x, core).
Axes of the slice: x: 4, y: 4, z: 4, core: 2. Of those that a mesh axis runs over, the one named last changes fastest.
Arguments:
- tokens: bfloat16 [1536, 8192], P('dp', 'tensor'), may hold values from -6 to 6
- cotangent: bfloat16 [1536, 8192], P('dp', 'tensor'), may hold values from -6 to 6
- gate_weight: bfloat16 [8192, 14336], P(None, 'tensor'), may hold values from -0.125 to 0.125
- up_weight: bfloat16 [8192, 14336], P(None, 'tensor'), may hold values from -0.125 to 0.125
- down_weight: bfloat16 [14336, 8192], P('tensor'), may hold values from -0.09375 to 0.09375
- block_task: int32 [12], P('dp'), may hold values from 0 to 63
- block_fill: int32 [12], P('dp'), may hold values from 1 to 128
- task_slot: int32 [64], replicated, may hold values from 0 to 63, each once
- inner_correction_weights: bfloat16 [64, 64, 8192], P('dp', None, 'tensor'), may hold values from -0.0625 to 0.0625
- up_b: bfloat16 [64, 64, 14336], P('dp', None, 'tensor'), may hold values from -0.75 to 0.75
Outputs:
- mixed: bfloat16 [1536, 8192], P('dp', 'tensor')
- item_derivative: bfloat16 [1536, 8192], P('dp', 'tensor')
- up_a_grad: bfloat16 [64, 64, 8192], P('dp', None, 'tensor')
- up_b_grad: bfloat16 [64, 64, 14336], P('dp', None, 'tensor')
Inputs may be any that keep to these rules, and one draw needn't show every extreme that they name: `task_slot`: slot s is held by data group s // 16.
All inputs are finite; a program needn't handle non-finite values.
Results may differ from a plain program's by a relative error of at most 0.019.
Values may be sent and summed in bfloat16 or wider, within the bound.
A program may use at most 128 MiB of HBM per device.

v0:
```python
import jax
import jax.numpy as jnp
from jax import lax
from jax.sharding import PartitionSpec as P

BLOCK = 128


adapter_scale = 0.25


def tensor_total(value):
    return lax.psum(value.astype(jnp.bfloat16), "tensor").astype(jnp.float32)


def common_result(value):
    return lax.psum_scatter(
        value.astype(jnp.bfloat16), "tensor", scatter_dimension=1, tiled=True
    ).astype(jnp.float32)


def body(
    tokens,
    cotangent,
    gate_weight,
    up_weight,
    down_weight,
    block_task,
    block_fill,
    task_slot,
    inner_correction_weights,
    up_b,
):
    row_count, local_width = tokens.shape
    block_count = block_task.shape[0]
    hidden_width = gate_weight.shape[1]
    task_ids = jnp.arange(task_slot.shape[0], dtype=jnp.int32)
    segment_owner_index = jnp.sum(
        jnp.where(block_task[:, None] == task_ids[None, :], task_slot[None, :], 0), axis=1
    )
    enabled_flags = (jnp.arange(BLOCK, dtype=jnp.int32)[None, :] < block_fill[:, None]).astype(
        jnp.float32
    )[..., None]
    complete_arrivals, every_out = (
        lax.all_gather(inner_correction_weights, "dp", axis=0, tiled=True),
        lax.all_gather(up_b, "dp", axis=0, tiled=True),
    )
    correction_source_vector = complete_arrivals[segment_owner_index]
    up_factor_output = every_out[segment_owner_index]
    piece = lax.all_gather(tokens, "tensor", axis=1, tiled=True)
    gating_piece = jnp.dot(piece, gate_weight, preferred_element_type=jnp.float32)
    expansion_running_total = jnp.dot(piece, up_weight, preferred_element_type=jnp.float32)
    d_hidden = lax.dot_general(
        lax.all_gather(cotangent, "tensor", axis=1, tiled=True),
        down_weight,
        (((1,), (1,)), ((), ())),
        preferred_element_type=jnp.float32,
    )
    portion_clusters = tokens.reshape(block_count, BLOCK, local_width)
    narrow_product = (
        tensor_total(
            jnp.einsum(
                "imk,iok->imo",
                portion_clusters,
                correction_source_vector,
                preferred_element_type=jnp.float32,
            )
        )
        * enabled_flags
    )
    low_rank_b_output = narrow_product.astype(jnp.bfloat16)
    adapter_up_output = jnp.einsum(
        "vam,vmk->vak", low_rank_b_output, up_factor_output, preferred_element_type=jnp.float32
    ).reshape(row_count, hidden_width)
    up_projection = expansion_running_total + adapter_scale * adapter_up_output
    sigmoid_gate = jax.nn.sigmoid(gating_piece)
    activated = gating_piece * sigmoid_gate
    hidden = (activated * up_projection).astype(jnp.bfloat16)
    mixed = common_result(jnp.dot(hidden, down_weight, preferred_element_type=jnp.float32)).astype(
        jnp.bfloat16
    )
    d_gate = (
        d_hidden * up_projection * sigmoid_gate * (1.0 + gating_piece * (1.0 - sigmoid_gate))
    ).astype(jnp.bfloat16)
    d_up = (d_hidden * activated).astype(jnp.bfloat16)
    gradient_per_block = d_up.reshape(block_count, BLOCK, hidden_width)
    narrow_derivative = (
        adapter_scale
        * tensor_total(
            jnp.einsum(
                "oge,oce->ogc",
                gradient_per_block,
                up_factor_output,
                preferred_element_type=jnp.float32,
            )
        )
        * enabled_flags
    )
    exterior_multiplier_dual = narrow_derivative.astype(jnp.bfloat16)
    contract = (((1,), (1,)), ((), ()))
    fixed_weight_derivative = lax.dot_general(
        d_gate, gate_weight, contract, preferred_element_type=jnp.float32
    )
    fixed_weight_derivative = fixed_weight_derivative + lax.dot_general(
        d_up, up_weight, contract, preferred_element_type=jnp.float32
    )
    adjoint_of_correction = jnp.einsum(
        "lxu,luz->lxz",
        exterior_multiplier_dual,
        correction_source_vector,
        preferred_element_type=jnp.float32,
    ).reshape(row_count, local_width)
    item_derivative = (common_result(fixed_weight_derivative) + adjoint_of_correction).astype(
        jnp.bfloat16
    )
    arriving_slope = jnp.einsum(
        "bqf,bqm->bfm",
        exterior_multiplier_dual,
        portion_clusters,
        preferred_element_type=jnp.float32,
    )
    output_gradient = adapter_scale * jnp.einsum(
        "wvd,wvg->wdg", low_rank_b_output, gradient_per_block, preferred_element_type=jnp.float32
    )
    slot_ids = jnp.arange(task_slot.shape[0], dtype=jnp.int32)
    one_hot = (segment_owner_index[:, None] == slot_ids[None, :]).astype(jnp.float32)
    spread_in = jnp.einsum("bs,brd->srd", one_hot, arriving_slope, precision=lax.Precision.HIGHEST)
    spread_out = jnp.einsum(
        "bs,brf->srf", one_hot, output_gradient, precision=lax.Precision.HIGHEST
    )
    owned_in, owned_out = (
        lax.psum_scatter(
            spread_in.astype(jnp.bfloat16), "dp", scatter_dimension=0, tiled=True
        ).astype(jnp.float32),
        lax.psum_scatter(
            spread_out.astype(jnp.bfloat16), "dp", scatter_dimension=0, tiled=True
        ).astype(jnp.float32),
    )
    return (mixed, item_derivative, owned_in.astype(jnp.bfloat16), owned_out.astype(jnp.bfloat16))


def solution(mesh):
    return jax.shard_map(
        body,
        mesh=mesh,
        in_specs=(
            P("dp", "tensor"),
            P("dp", "tensor"),
            P(None, "tensor"),
            P(None, "tensor"),
            P("tensor", None),
            P("dp"),
            P("dp"),
            P(),
            P("dp", None, "tensor"),
            P("dp", None, "tensor"),
        ),
        out_specs=(
            P("dp", "tensor"),
            P("dp", "tensor"),
            P("dp", None, "tensor"),
            P("dp", None, "tensor"),
        ),
        check_vma=False,
    )
```

profile of v0, /device:TPU:1, one launch (start us, length us, event | category | flops | bytes accessed | tf_op | source)
XLA Modules:
  0.0 580.6 jit_solution(4219731745124527441)
XLA Ops:
  7.2 0.0 all-gather.7.cloned.1.call-start
  7.2 0.7 all-gather.7.cloned.1.call-update
  7.9 0.0 all-gather.9.cloned.1.call-start
  7.9 0.7 all-gather.9.cloned.1.call-update
  8.7 0.0 all-gather.5.cloned.1.call-start
  8.7 0.7 all-gather.5.cloned.1.call-update
  9.4 0.0 all-gather.11.cloned.1.call-start
  9.4 0.5 all-gather.11.cloned.1.call-update
  10.0 0.0 all-reduce.3.cloned.1.call-start
  10.0 0.9 select_reduce_fusion
  10.9 32.6 %all-gather.7.cloned.1.call-done = bf16[64,64,256]{2,1,0:T(8,128)(2,1)} async-done(((bf16[16,64,256]{2,1,0:T(8,128)(2,1)}), bf16[64,64,256]{2,1,0:T(8,128)(2,1)}) %all-gather.7.cloned.1.call-update) | async-done | bytes 2097168 | tf_op jit(solution)/shard_map/all_gather | solution.py:45
  43.5 2.1 gather_fusion
  45.6 1.7 fusion
  47.4 46.0 %all-gather.9.cloned.1.call-done = bf16[64,64,448]{2,1,0:T(8,128)(2,1)} async-done(((bf16[16,64,448]{2,1,0:T(8,128)(2,1)}), bf16[64,64,448]{2,1,0:T(8,128)(2,1)}) %all-gather.9.cloned.1.call-update) | async-done | bytes 3670032 | tf_op jit(solution)/shard_map/all_gather | solution.py:46
  93.4 2.7 gather_fusion.1
  96.2 54.1 %all-gather.5.cloned.1.call-done = bf16[384,8192]{1,0:T(8,128)(2,1)} async-done(((bf16[384,256]{1,0:T(8,128)(2,1)}), bf16[384,8192]{1,0:T(8,128)(2,1)}) %all-gather.5.cloned.1.call-update) | async-done | bytes 6291472 | tf_op jit(solution)/shard_map/all_gather | solution.py:50
  150.3 8.4 %fusion.20 = f32[384,448]{0,1:T(8,128)S(1)} fusion(bf16[384,8192]{1,0:T(8,128)(2,1)} %all-gather.5.cloned.1.call-done, bf16[8192,448]{0,1:T(8,128)(2,1)} %param.12), kind=kOutput, calls=%fused_computation.41 | convolution fusion | flops 2818572288 | bytes 14319616 | tf_op jit(solution)/shard_map/dot_general | solution.py:51
  158.7 0.0 copy-start.3
  158.7 0.0 copy-start
  158.7 46.9 %all-gather.11.cloned.1.call-done = bf16[384,8192]{1,0:T(8,128)(2,1)} async-done(((bf16[384,256]{1,0:T(8,128)(2,1)}), bf16[384,8192]{1,0:T(8,128)(2,1)}) %all-gather.11.cloned.1.call-update) | async-done | bytes 6291472 | tf_op jit(solution)/shard_map/all_gather | solution.py:54
  205.6 8.4 %multiply_convert_fusion = (bf16[384,448]{0,1:T(8,128)(2,1)S(1)}, f32[384,448]{0,1:T(8,128)S(1)}) fusion(f32[384,448]{0,1:T(8,128)S(1)} %fusion.20, bf16[384,8192]{1,0:T(8,128)(2,1)} %all-gather.11.cloned.1.call-done, bf16[448,8192]{1,0:T(8,128)(2,1)} %param.14), kind=kOutput, calls=%fused_computation.12 | convolution fusion | flops 2819604480 | bytes 15351808 | tf_op jit(solution)/shard_map/dot_general | solution.py:53
  214.0 0.2 copy.35
  214.2 0.9 convolution_convert_fusion.4
  215.1 0.0 all-reduce.3.cloned.1.call-update
  215.1 0.0 reduce-scatter.9.cloned.1.call-start
  215.2 0.0 copy-done.3
  215.2 0.1 fusion.10
  215.2 98.2 %all-reduce.3.cloned.1.call-done = (bf16[3,128,64]{1,2,0:T(8,128)(2,1)}, bf16[3,128,64]{1,2,0:T(8,128)(2,1)}) async-done(((bf16[3,128,64]{1,2,0:T(8,128)(2,1)}, bf16[3,128,64]{1,2,0:T(8,128)(2,1)}), (bf16[3,128,64]{1,2,0:T(8,128)(2,1)}, bf16[3,128,64]{1,2,0:T(8,128)(2,1)})) %all-reduce.3.cloned.1.call-update) | async-done | bytes 98320 | tf_op jit(solution)/shard_map/psum | solution.py:13
  313.5 0.0 copy-start.1
  313.5 0.0 copy-done
  313.5 1.0 fusion.8
  314.4 3.3 convolution_convert_fusion.2
  317.7 0.0 reduce-scatter.9.cloned.1.call-update
  317.7 0.0 reduce-scatter.11.cloned.1.call-start
  317.8 0.1 fusion.11
  317.9 1.0 convolution_multiply_fusion.1
  318.9 5.3 convolution_convert_fusion.1
  324.1 0.0 reduce-scatter.11.cloned.1.call-update
  324.1 0.2 reduce-scatter.7.cloned.1.call-start
  324.4 0.0 copy-done.1
  324.4 0.3 convolution_multiply_fusion
  324.7 0.3 copy.33
  325.0 0.2 copy.34
  325.2 8.9 %convolution_add_fusion = f32[384,448]{0,1:T(8,128)S(1)} fusion(f32[384,448]{0,1:T(8,128)S(1)} %copy.34, bf16[384,8192]{1,0:T(8,128)(2,1)} %all-gather.5.cloned.1.call-done, bf16[8192,448]{0,1:T(8,128)(2,1)} %param.13), kind=kOutput, calls=%fused_computation.7 | convolution fusion | flops 2818744320 | bytes 15007744 | tf_op jit(solution)/shard_map/dot_general | solution.py:52
  334.1 6.1 %fusion.4 = f32[384,8192]{1,0:T(8,128)S(1)} fusion(bf16[8192,448]{0,1:T(8,128)(2,1)} %param.12, f32[384,448]{0,1:T(8,128)S(1)} %fusion.20, f32[384,448]{0,1:T(8,128)S(1)} %get-tuple-element.23, f32[384,448]{0,1:T(8,128)S(1)} %convolution_add_fusion), kind=kOutput, calls=%fused_computation.20 | convolution fusion | flops 2820292608 | bytes 21987328 | tf_op jit(solution)/shard_map/dot_general | solution.py:101
  340.2 9.8 %add_convert_fusion = bf16[384,8192]{1,0:T(8,128)(2,1)} fusion(f32[384,8192]{1,0:T(8,128)S(1)} %fusion.4, bf16[384,448]{0,1:T(8,128)(2,1)S(1)} %get-tuple-element.22, bf16[8192,448]{0,1:T(8,128)(2,1)} %param.13), kind=kOutput, calls=%fused_computation.2 | convolution fusion | flops 2824863744 | bytes 26558464 | tf_op jit(solution)/shard_map/dot_general | solution.py:104
  349.9 0.0 reduce-scatter.7.cloned.1.call-update
  349.9 0.0 copy-start.2
  350.0 0.3 reduce-scatter.5.cloned.1.call-start
  350.2 9.5 %convolution_convert_fusion = bf16[384,8192]{1,0:T(8,128)(2,1)} fusion(bf16[448,8192]{1,0:T(8,128)(2,1)} %param.14, f32[384,448]{0,1:T(8,128)S(1)} %convolution_add_fusion, f32[384,448]{0,1:T(8,128)S(1)} %fusion.20), kind=kOutput, calls=%fused_computation.3 | convolution fusion | flops 2822750208 | bytes 15007744 | tf_op jit(solution)/shard_map/dot_general | solution.py:79
  359.7 0.0 reduce-scatter.5.cloned.1.call-update
  359.7 0.0 copy-done.2
  359.7 0.3 fusion.9
  360.0 0.0 reduce-scatter.9.cloned.1.call-done
  360.0 2.0 copy.40
  362.0 33.9 %reduce-scatter.11.cloned.1.call-done = bf16[16,64,448]{2,0,1:T(8,128)(2,1)} async-done(((bf16[64,64,448]{2,0,1:T(8,128)(2,1)}), bf16[16,64,448]{2,0,1:T(8,128)(2,1)}) %reduce-scatter.11.cloned.1.call-update) | async-done | bytes 917520 | tf_op jit(solution)/shard_map/reduce_scatter | solution.py:135
  395.9 2.8 copy.41
  398.7 85.4 %reduce-scatter.7.cloned.1.call-done = bf16[384,256]{1,0:T(8,128)(2,1)} async-done(((bf16[384,8192]{1,0:T(8,128)(2,1)}), bf16[384,256]{1,0:T(8,128)(2,1)}) %reduce-scatter.7.cloned.1.call-update) | async-done | bytes 196624 | tf_op jit(solution)/shard_map/reduce_scatter | solution.py:17
  484.1 1.7 fusion.3
  485.7 88.3 %reduce-scatter.5.cloned.1.call-done = bf16[384,256]{1,0:T(8,128)(2,1)} async-done(((bf16[384,8192]{1,0:T(8,128)(2,1)}), bf16[384,256]{1,0:T(8,128)(2,1)}) %reduce-scatter.5.cloned.1.call-update) | async-done | bytes 196624 | tf_op jit(solution)/shard_map/reduce_scatter | solution.py:17
  (2 shorter events, 0.0 us)
Async XLA Ops:
  7.2 36.3 %all-gather.7.cloned.1.call-start = ((), (), s32[]{:S(2)}) async-start(), calls=%async_computation.5 | async-start | bytes 2621440 | tf_op jit(solution)/shard_map/all_gather | solution.py:45
  7.9 85.5 %all-gather.9.cloned.1.call-start = ((), (), s32[]{:S(2)}) async-start(), calls=%async_computation.6 | async-start | bytes 5242880 | tf_op jit(solution)/shard_map/all_gather | solution.py:46
  8.7 141.6 %all-gather.5.cloned.1.call-start = ((), (), s32[]{:S(2)}) async-start(), calls=%async_computation.4 | async-start | bytes 6488064 | tf_op jit(solution)/shard_map/all_gather | solution.py:50
  9.4 196.2 %all-gather.11.cloned.1.call-start = ((), (), s32[]{:S(2)}) async-start(), calls=%async_computation.8 | async-start | bytes 6488064 | tf_op jit(solution)/shard_map/all_gather | solution.py:54
  10.0 303.5 %all-reduce.3.cloned.1.call-start = ((), (), s32[]{:S(2)}) async-start(), calls=%async_computation.12 | async-start | bytes 196608 | tf_op jit(solution)/shard_map/psum | solution.py:13
  158.7 56.5 %copy-start.3 = (s32[3]{0:T(128)S(1)}, s32[3]{0:T(128)}, u32[]{:S(2)}) copy-start(s32[3]{0:T(128)} %param.16) | copy-start | bytes 40
  158.7 154.8 %copy-start = (bf16[384,256]{1,0:T(8,128)(2,1)S(1)}, bf16[384,256]{1,0:T(8,128)(2,1)}, u32[]{:S(2)}) copy-start(bf16[384,256]{1,0:T(8,128)(2,1)} %param.10) | copy-start | bytes 589828
  215.1 144.9 %reduce-scatter.9.cloned.1.call-start = ((), (), s32[]{:S(2)}) async-start(), calls=%async_computation.10 | async-start | bytes 2621440 | tf_op jit(solution)/shard_map/reduce_scatter | solution.py:132
  313.5 10.9 %copy-start.1 = (bf16[3,128,64]{1,2,0:T(8,128)(2,1)S(1)}, bf16[3,128,64]{1,2,0:T(8,128)(2,1)}, u32[]{:S(2)}) copy-start(bf16[3,128,64]{1,2,0:T(8,128)(2,1)} %get-tuple-element.20) | copy-start | bytes 147460
  317.7 78.2 %reduce-scatter.11.cloned.1.call-start = ((), (), s32[]{:S(2)}) async-start(), calls=%async_computation.11 | async-start | bytes 5242880 | tf_op jit(solution)/shard_map/reduce_scatter | solution.py:135
  324.1 160.0 %reduce-scatter.7.cloned.1.call-start = ((), (), s32[]{:S(2)}) async-start(), calls=%async_computation.9 | async-start | bytes 6488064 | tf_op jit(solution)/shard_map/reduce_scatter | solution.py:17
  349.9 9.8 %copy-start.2 = (bf16[3,128,64]{1,2,0:T(8,128)(2,1)S(1)}, bf16[3,128,64]{1,2,0:T(8,128)(2,1)}, u32[]{:S(2)}) copy-start(bf16[3,128,64]{1,2,0:T(8,128)(2,1)} %get-tuple-element.21) | copy-start | bytes 147460
  350.0 224.1 %reduce-scatter.5.cloned.1.call-start = ((), (), s32[]{:S(2)}) async-start(), calls=%async_computation.7 | async-start | bytes 6488064 | tf_op jit(solution)/shard_map/reduce_scatter | solution.py:17
Sparse Core Ops, SparseCore 0:
  9.6 33.8 all-gather.6
  45.2 48.2 all-gather.8
  95.6 54.6 all-gather.4
  152.3 53.2 all-gather.10
  215.2 98.1 all-reduce.2
  317.8 29.0 reduce-scatter.8
  349.3 46.5 reduce-scatter.10
  399.6 84.4 reduce-scatter.6
  488.4 85.5 reduce-scatter.4
where the time goes:
time: 582 us; the launch traced here: 581 us
  waiting for transfers between devices  488 us (84%)
  matrix products  64.7 us (11%)
  between operations  14 us (2%)
  local copies, waits for them, and re-layouts  10.4 us (2%)
    reduce_scatter x2, waiting for transfers between devices, common_result(): lax.psum_scatter(value.astype(jnp.bfloat16), 'tensor', scatter_dimension=...  174 us
    psum x1, waiting for transfers between devices, tensor_total(): return lax.psum(value.astype(jnp.bfloat16), 'tensor').astype(jnp.float32)  98.2 us
    all_gather x1, waiting for transfers between devices, body(): piece = lax.all_gather(tokens, 'tensor', axis=1, tiled=True)  54.1 us
    all_gather x1, waiting for transfers between devices, body(): lax.all_gather(cotangent, 'tensor', axis=1, tiled=True)  46.9 us
    all_gather x1, waiting for transfers between devices, body(): lax.all_gather(up_b, 'dp', axis=0, tiled=True)  46 us
    reduce_scatter x1, waiting for transfers between devices, body(): lax.psum_scatter(spread_out.astype(jnp.bfloat16), 'dp', scatter_dimension...  33.9 us
    all_gather x1, waiting for transfers between devices, body(): lax.all_gather(inner_correction_weights, 'dp', axis=0, tiled=True)  32.6 us
  transfers between devices with their start and end apart: 9, of which 8 were waited for; matrix products, arithmetic and copies ran while one was open for 11% of the time, Pallas kernels for 0%

commit v1 on v0

--- a/solution.py
+++ b/solution.py
@@ -1,22 +1,426 @@
+import functools
+
 import jax
 import jax.numpy as jnp
 from jax import lax
+from jax.experimental import pallas as pl
+from jax.experimental.pallas import tpu as pltpu
 from jax.sharding import PartitionSpec as P
 
 BLOCK = 128
-
+SIDE = 4
+CHIPS = SIDE * SIDE
+MESH = pl.DeviceIdType.MESH
+LAG = 6
+
+GATHER_ORDER = (0, 4, 1, 8, 2, 12, 3, 5, 6, 9, 10, 13, 7, 14, 11, 15)
+SCATTER_ORDER = (15, 14, 11, 13, 7, 12, 3, 10, 9, 6, 8, 2, 5, 4, 1, 0)
 
 adapter_scale = 0.25
+
+
+def pick(table, step):
+    value = jnp.int32(table[0])
+    for k in range(1, len(table)):
+        value = jnp.where(step == k, jnp.int32(table[k]), value)
+    return value
+
+
+def shifted(position, offset, sign):
+    delta = jnp.where(offset == 1, -sign, 0) + jnp.where(offset == 2, sign, 0) + jnp.where(offset == 3, 2, 0)
+    return lax.rem(position + delta + SIDE, SIDE)
+
+
+def layer_kernel(
+    tokens_ref,
+    cotangent_ref,
+    gate_hbm,
+    up_hbm,
+    down_hbm,
+    extra_ref,
+    mixed_ref,
+    item_ref,
+    d_up_ref,
+    gathered,
+    gate_w,
+    up_w,
+    down_w,
+    gate_acc,
+    up_acc,
+    dh_acc,
+    hidden,
+    d_gate,
+    to_partner,
+    parts,
+    landed,
+    own_sem,
+    weight_sem,
+    ag_send,
+    ag_recv,
+    pair_send,
+    pair_recv,
+    half_send,
+    half_recv,
+    rs_send,
+    rs_recv,
+):
+    rows, width = tokens_ref.shape
+    hidden_width = gate_acc.shape[1]
+    part_rows = rows // 2
+    me = lax.axis_index("tensor")
+    core = lax.rem(me, 2)
+    x = lax.rem(me // 2, SIDE)
+    z = me // (2 * SIDE)
+    sign = 1 - 2 * core
+    partner = me + sign
+
+    def index(zz, xx, cc):
+        return (zz * SIDE + xx) * 2 + cc
+
+    x_up = index(z, lax.rem(x + sign + SIDE, SIDE), core)
+    x_down = index(z, lax.rem(x - sign + SIDE, SIDE), core)
+    z_up = index(lax.rem(z + sign + SIDE, SIDE), x, core)
+    z_down = index(lax.rem(z - sign + SIDE, SIDE), x, core)
+    along = {"x": (x_up, x_down), "z": (z_up, z_down)}
+
+    def mine(idx):
+        return index(shifted(z, idx % SIDE, sign), shifted(x, idx // SIDE, sign), core)
+
+    def theirs(idx):
+        return index(shifted(z, idx % SIDE, -sign), shifted(x, idx // SIDE, -sign), 1 - core)
+
+    def remote(src, dst, send, recv, to):
+        return pltpu.make_async_remote_copy(
+            src_ref=src, dst_ref=dst, send_sem=send, recv_sem=recv, device_id={"tensor": to}, device_id_type=MESH
+        )
+
+    barrier = pltpu.get_barrier_semaphore()
+    for peer in (partner, x_up, x_down, z_up, z_down):
+        pl.semaphore_signal(barrier, inc=1, device_id={"tensor": peer}, device_id_type=MESH)
+
+    own = [
+        pltpu.make_async_copy(ref, gathered.at[a, me], own_sem.at[a])
+        for a, ref in enumerate((tokens_ref, cotangent_ref))
+    ]
+    for copy in own:
+        copy.start()
+
+    def weight_copies(shard):
+        at = pl.multiple_of(shard * width, width)
+        return (
+            pltpu.make_async_copy(gate_hbm.at[:, pl.ds(at, width)], gate_w.at[shard], weight_sem.at[0, shard]),
+            pltpu.make_async_copy(up_hbm.at[:, pl.ds(at, width)], up_w.at[shard], weight_sem.at[1, shard]),
+            pltpu.make_async_copy(down_hbm.at[:, pl.ds(at, width)], down_w.at[shard], weight_sem.at[2, shard]),
+        )
+
+    pl.semaphore_wait(barrier, 5)
+
+    half = (slice(0, part_rows), slice(part_rows, rows))
+
+    def ag_copy(a, h, shard, idx, to):
+        ref = gathered.at[a, shard, half[h], :]
+        return remote(ref, ref, ag_send.at[a, h, idx], ag_recv.at[a, h, idx], to)
+
+    def arrive(a, idx, first):
+        ox, oz = idx // SIDE, idx % SIDE
+        shard = mine(idx)
+        if first:
+            own[a].wait()
+        for h, (name_f, name_g) in enumerate((("x", "z"), ("z", "x"))):
+            of, og = (ox, oz) if h == 0 else (oz, ox)
+
+            def spot(f, g, h=h):
+                return f * SIDE + g if h == 0 else g * SIDE + f
+
+            if not first:
+                ag_copy(a, h, shard, idx, x_up).wait_recv()
+            f_up, f_down = along[name_f]
+            g_up, g_down = along[name_g]
+            if first:
+                ag_copy(a, h, shard, spot(1, 0), f_up).start()
+                ag_copy(a, h, shard, spot(2, 0), f_down).start()
+                ag_copy(a, h, shard, spot(0, 1), g_up).start()
+                ag_copy(a, h, shard, spot(0, 2), g_down).start()
+            else:
+
+                @pl.when(jnp.logical_and(og == 0, of == 1))
+                def _():
+                    ag_copy(a, h, shard, spot(3, 0), f_up).start()
+
+                @pl.when(og == 0)
+                def _():
+                    ag_copy(a, h, shard, spot(of, 1), g_up).start()
+                    ag_copy(a, h, shard, spot(of, 2), g_down).start()
+
+                @pl.when(og == 1)
+                def _():
+                    ag_copy(a, h, shard, spot(of, 3), g_up).start()
+
+        pair_copy(a, shard, idx).start()
+
+    def pair_copy(a, shard, idx):
+        ref = gathered.at[a, shard]
+        return remote(ref, ref, pair_send.at[a, idx], pair_recv.at[a, idx], partner)
+
+    arrive(0, jnp.int32(0), True)
+
+    def start_weights(kind):
+        def at_step(k, carry):
+            idx = pick(GATHER_ORDER, k)
+            for shard in (mine(idx), theirs(idx)):
+                copies = weight_copies(shard)
+                for copy in copies[:2] if kind == 0 else copies[2:]:
+                    copy.start()
+            return carry
+
+        lax.fori_loop(0, CHIPS, at_step, 0)
+
+    start_weights(0)
+    start_weights(1)
+    gate_acc[...] = jnp.zeros_like(gate_acc)
+    up_acc[...] = jnp.zeros_like(up_acc)
+    dh_acc[...] = jnp.zeros_like(dh_acc)
+
+    across = (((1,), (1,)), ((), ()))
+
+    def use(a, shard):
+        copies = weight_copies(shard)
+        if a == 0:
+            copies[0].wait()
+            copies[1].wait()
+            piece = gathered[0, shard]
+            gate_acc[...] += lax.dot_general(piece, gate_w[shard], across, preferred_element_type=jnp.float32)
+            up_acc[...] += lax.dot_general(piece, up_w[shard], across, preferred_element_type=jnp.float32)
+        else:
+            copies[2].wait()
+            dh_acc[...] += lax.dot_general(
+                gathered[1, shard], down_w[shard], across, preferred_element_type=jnp.float32
+            )
+
+    def visit(a, k):
+        @pl.when(jnp.logical_and(k >= 1, k < CHIPS))
+        def _():
+            arrive(a, pick(GATHER_ORDER, k), False)
+
+        for which in (0, 1):
+
+            @pl.when(k < CHIPS if which == 0 else jnp.logical_and(k >= 1, k < CHIPS + 1))
+            def _():
+                idx = pick(GATHER_ORDER, k - which)
+                if which == 0:
+                    shard = mine(idx)
+                else:
+                    shard = theirs(idx)
+                    pair_copy(a, shard, idx).wait_recv()
+                use(a, shard)
+
+    def gather_step(k, carry):
+        @pl.when(k == LAG)
+        def _():
+            arrive(1, jnp.int32(0), True)
+
+        @pl.when(k < CHIPS + 1)
+        def _():
+            visit(0, k)
+
+        @pl.when(k >= LAG)
+        def _():
+            visit(1, k - LAG)
+
+        return carry
+
+    lax.fori_loop(0, CHIPS + 1 + LAG, gather_step, 0)
+
+    def middle(block, carry):
+        at = pl.ds(pl.multiple_of(block * 64, 64), 64)
+        gate = gate_acc[at, :]
+        up = up_acc[at, :] + adapter_scale * extra_ref[at, :]
+        d_hidden = dh_acc[at, :]
+        sigmoid_gate = jax.nn.sigmoid(gate)
+        activated = gate * sigmoid_gate
+        hidden[at, :] = (activated * up).astype(jnp.bfloat16)
+        d_gate[at, :] = (d_hidden * up * sigmoid_gate * (1.0 + gate * (1.0 - sigmoid_gate))).astype(jnp.bfloat16)
+        d_up_ref[at, :] = (d_hidden * activated).astype(jnp.bfloat16)
+        return carry
+
+    lax.fori_loop(0, rows // 64, middle, 0)
+
+    def product(r, shard):
+        if r == 0:
+            return jnp.dot(hidden[...], down_w[shard], preferred_element_type=jnp.float32)
+        return jnp.dot(d_gate[...], gate_w[shard], preferred_element_type=jnp.float32) + jnp.dot(
+            d_up_ref[...], up_w[shard], preferred_element_type=jnp.float32
+        )
+
+    def half_copy(r, idx):
+        return remote(to_partner.at[idx], parts.at[r, idx], half_send.at[r, idx], half_recv.at[r, idx], partner)
+
+    def rs_copy(r, h, idx, slot, to):
+        return remote(parts.at[r, idx, half[h], :], landed.at[r, h, slot], rs_send.at[r, h, slot], rs_recv.at[r, h, slot], to)
+
+    names = (("z", "x"), ("x", "z"))
+
+    def place(h, f, g):
+        return g * SIDE + f if h == 0 else f * SIDE + g
+
+    def produce(r, k):
+        @pl.when(k < CHIPS)
+        def _():
+            idx = pick(SCATTER_ORDER, k)
+            if r == 1:
+                half_copy(0, idx).wait_send()
+            to_partner[idx] = product(r, theirs(idx)).astype(jnp.bfloat16)
+            half_copy(r, idx).start()
+
+        @pl.when(k >= 2)
+        def _():
+            idx = pick(SCATTER_ORDER, k - 2)
+            half_copy(r, idx).wait_recv()
+            parts[r, idx] = (product(r, mine(idx)) + parts[r, idx].astype(jnp.float32)).astype(jnp.bfloat16)
+            ox, oz = idx // SIDE, idx % SIDE
+            for h in (0, 1):
+                of, og = (oz, ox) if h == 0 else (ox, oz)
+                f_up, f_down = along[names[h][0]]
+
+                @pl.when(of == 3)
+                def _():
+                    rs_copy(r, h, idx, og, f_down).start()
+
+                @pl.when(of == 2)
+                def _():
+                    rs_copy(r, h, idx, SIDE + og, f_up).start()
+
+    def add_in(r, h, idx, slots, out=None):
+        for slot in slots:
+            rs_copy(r, h, idx, slot, x_up).wait_recv()
+        total = parts[r, idx, half[h], :].astype(jnp.float32)
+        for slot in slots:
+            total = total + landed[r, h, slot].astype(jnp.float32)
+        if out is None:
+            parts[r, idx, half[h], :] = total.astype(jnp.bfloat16)
+        else:
+            out[half[h], :] = total.astype(out.dtype)
+
+    def combine(r, h, g):
+        idx = place(h, 1, g)
+        add_in(r, h, idx, (g,))
+        rs_copy(r, h, idx, 2 * SIDE + g, along[names[h][0]][1]).start()
+
+    def finish(r, h, g):
+        idx = place(h, 0, g)
+        add_in(r, h, idx, (SIDE + g, 2 * SIDE + g))
+        g_up, g_down = along[names[h][1]]
+        if g == 3:
+            rs_copy(r, h, idx, 3 * SIDE, g_down).start()
+        elif g == 2:
+            rs_copy(r, h, idx, 3 * SIDE + 1, g_up).start()
+        elif g == 1:
+            add_in(r, h, idx, (3 * SIDE,))
+            rs_copy(r, h, idx, 3 * SIDE + 2, g_down).start()
+        else:
+            add_in(r, h, idx, (3 * SIDE + 1, 3 * SIDE + 2), (mixed_ref, item_ref)[r])
+
+    def mixed_step(k, carry):
+        produce(0, k)
+        return carry
+
+    lax.fori_loop(0, CHIPS + 2, mixed_step, 0)
+
+    def item_step(k, carry):
+        produce(1, k)
+        for n, g in enumerate((3, 2, 1, 0)):
+
+            @pl.when(k == 1 + 2 * n)
+            def _():
+                combine(0, 0, g)
+                combine(0, 1, g)
+
+            @pl.when(k == 10 + 2 * n)
+            def _():
+                finish(0, 0, g)
+                finish(0, 1, g)
+
+        return carry
+
+    lax.fori_loop(0, CHIPS + 2, item_step, 0)
+    for g in (3, 2, 1, 0):
+        combine(1, 0, g)
+        combine(1, 1, g)
+    for g in (3, 2, 1, 0):
+        finish(1, 0, g)
+        finish(1, 1, g)
+
+    def drain(k, carry):
+        for a in (0, 1):
+            pair_copy(a, me, k).wait_send()
+
+            @pl.when(k >= 1)
+            def _():
+                for h in (0, 1):
+                    ag_copy(a, h, me, k, x_up).wait_send()
+
+            @pl.when(k < 15)
+            def _():
+                for h in (0, 1):
+                    rs_copy(a, h, k, k, x_up).wait_send()
+
+        half_copy(1, k).wait_send()
+        return carry
+
+    lax.fori_loop(0, CHIPS, drain, 0)
+
+
+def layer(tokens, cotangent, gate_weight, up_weight, down_weight, extra):
+    rows, width = tokens.shape
+    hidden_width = gate_weight.shape[1]
+    shards = gate_weight.shape[0] // width
+    half = rows // 2
+    any_spec = pl.BlockSpec(memory_space=pl.ANY)
+    vmem_spec = pl.BlockSpec(memory_space=pltpu.VMEM)
+    bf16, f32 = jnp.bfloat16, jnp.float32
+    dma = pltpu.SemaphoreType.DMA
+    return pl.pallas_call(
+        layer_kernel,
+        out_shape=(
+            jax.ShapeDtypeStruct((rows, width), bf16),
+            jax.ShapeDtypeStruct((rows, width), f32),
+            jax.ShapeDtypeStruct((rows, hidden_width), bf16),
+        ),
+        in_specs=[any_spec] * 5 + [vmem_spec],
+        out_specs=(vmem_spec,) * 3,
+        scratch_shapes=[
+            pltpu.VMEM((2, shards, rows, width), bf16),
+            pltpu.VMEM((shards, hidden_width, width), bf16),
+            pltpu.VMEM((shards, hidden_width, width), bf16),
+            pltpu.VMEM((shards, hidden_width, width), bf16),
+            pltpu.VMEM((rows, hidden_width), f32),
+            pltpu.VMEM((rows, hidden_width), f32),
+            pltpu.VMEM((rows, hidden_width), f32),
+            pltpu.VMEM((rows, hidden_width), bf16),
+            pltpu.VMEM((rows, hidden_width), bf16),
+            pltpu.VMEM((CHIPS, rows, width), bf16),
+            pltpu.VMEM((2, CHIPS, rows, width), bf16),
+            pltpu.VMEM((2, 2, 15, half, width), bf16),
+            dma((2,)),
+            dma((3, shards)),
+            dma((2, 2, CHIPS)),
+            dma((2, 2, CHIPS)),
+            dma((2, CHIPS)),
+            dma((2, CHIPS)),
+            dma((2, CHIPS)),
+            dma((2, CHIPS)),
+            dma((2, 2, 15)),
+            dma((2, 2, 15)),
+        ],
+        compiler_params=pltpu.CompilerParams(
+            collective_id=0, has_side_effects=True, vmem_limit_bytes=67043328
+        ),
+        name="layer",
+    )(tokens, cotangent, gate_weight.T, up_weight.T, down_weight, extra)
 
 
 def tensor_total(value):
     return lax.psum(value.astype(jnp.bfloat16), "tensor").astype(jnp.float32)
-
-
-def common_result(value):
-    return lax.psum_scatter(
-        value.astype(jnp.bfloat16), "tensor", scatter_dimension=1, tiled=True
-    ).astype(jnp.float32)
 
 
 def body(
@@ -47,15 +451,6 @@
     )
     correction_source_vector = complete_arrivals[segment_owner_index]
     up_factor_output = every_out[segment_owner_index]
-    piece = lax.all_gather(tokens, "tensor", axis=1, tiled=True)
-    gating_piece = jnp.dot(piece, gate_weight, preferred_element_type=jnp.float32)
-    expansion_running_total = jnp.dot(piece, up_weight, preferred_element_type=jnp.float32)
-    d_hidden = lax.dot_general(
-        lax.all_gather(cotangent, "tensor", axis=1, tiled=True),
-        down_weight,
-        (((1,), (1,)), ((), ())),
-        preferred_element_type=jnp.float32,
-    )
     portion_clusters = tokens.reshape(block_count, BLOCK, local_width)
     narrow_product = (
         tensor_total(
@@ -72,17 +467,7 @@
     adapter_up_output = jnp.einsum(
         "vam,vmk->vak", low_rank_b_output, up_factor_output, preferred_element_type=jnp.float32
     ).reshape(row_count, hidden_width)
-    up_projection = expansion_running_total + adapter_scale * adapter_up_output
-    sigmoid_gate = jax.nn.sigmoid(gating_piece)
-    activated = gating_piece * sigmoid_gate
-    hidden = (activated * up_projection).astype(jnp.bfloat16)
-    mixed = common_result(jnp.dot(hidden, down_weight, preferred_element_type=jnp.float32)).astype(
-        jnp.bfloat16
-    )
-    d_gate = (
-        d_hidden * up_projection * sigmoid_gate * (1.0 + gating_piece * (1.0 - sigmoid_gate))
-    ).astype(jnp.bfloat16)
-    d_up = (d_hidden * activated).astype(jnp.bfloat16)
+    mixed, fixed, d_up = layer(tokens, cotangent, gate_weight, up_weight, down_weight, adapter_up_output)
     gradient_per_block = d_up.reshape(block_count, BLOCK, hidden_width)
     narrow_derivative = (
         adapter_scale
@@ -97,22 +482,13 @@
         * enabled_flags
     )
     exterior_multiplier_dual = narrow_derivative.astype(jnp.bfloat16)
-    contract = (((1,), (1,)), ((), ()))
-    fixed_weight_derivative = lax.dot_general(
-        d_gate, gate_weight, contract, preferred_element_type=jnp.float32
-    )
-    fixed_weight_derivative = fixed_weight_derivative + lax.dot_general(
-        d_up, up_weight, contract, preferred_element_type=jnp.float32
-    )
     adjoint_of_correction = jnp.einsum(
         "lxu,luz->lxz",
         exterior_multiplier_dual,
         correction_source_vector,
         preferred_element_type=jnp.float32,
     ).reshape(row_count, local_width)
-    item_derivative = (common_result(fixed_weight_derivative) + adjoint_of_correction).astype(
-        jnp.bfloat16
-    )
+    item_derivative = (fixed + adjoint_of_correction).astype(jnp.bfloat16)
     arriving_slope = jnp.einsum(
         "bqf,bqm->bfm",
         exterior_multiplier_dual,

time: 582 us -> 489 us (0.84)
  waiting for transfers between devices: 488 us -> 103 us
  blocking collectives: 0 us -> 245 us
  Pallas kernels: 0 us -> 97.4 us
  matrix products: 64.7 us -> 14.4 us
    psum x0 -> x2, blocking collectives: none -> 245 us  [tensor_total(): return lax.psum(value.astype(jnp.bfloat16), 'tensor').astype(jnp.float32)]
    reduce_scatter x2 -> x0, waiting for transfers between devices: 174 us -> none  [common_result(): lax.psum_scatter(value.astype(jnp.bfloat16), 'tensor', scatter_dimension=...]
    all_gather x2 -> x0, waiting for transfers between devices: 101 us -> none  [the longest x1 54.1 us: body(): piece = lax.all_gather(tokens, 'tensor', axis=1, tiled=True)]
    psum x1 -> x0, waiting for transfers between devices: 98.2 us -> none  [tensor_total(): return lax.psum(value.astype(jnp.bfloat16), 'tensor').astype(jnp.float32)]
    pallas_call x0 -> x1, Pallas kernels: none -> 97.4 us  [layer(): pl.pallas_call(layer_kernel, out_shape=(jax.ShapeDtypeStruct((rows, width...]
    dot_general x6 -> x0, matrix products: 51 us -> none  [the longest x1 9.76 us: body(): lax.dot_general(d_up, up_weight, contract, preferred_element_type=jnp.flo...]
    all_gather x1, waiting for transfers between devices: 46 us -> 0.01 us  [body(): lax.all_gather(up_b, 'dp', axis=0, tiled=True)]
    reduce_scatter x1, waiting for transfers between devices: 0.02 us -> 23 us  [body(): lax.psum_scatter(spread_in.astype(jnp.bfloat16), 'dp', scatter_dimension=...]
  transfers between devices with their start and end apart: 9 -> 4, of which waited for: 8 -> 3; matrix products, arithmetic and copies ran while one was open for 11% -> 3% of each run, Pallas kernels for 0% -> 0%
where the time goes in v1:
time: 489 us; the launch traced here: 488 us
  blocking collectives  245 us (50%)
  waiting for transfers between devices  103 us (21%)
  Pallas kernels  97.4 us (20%)
  matrix products  14.4 us (3%)
  between operations  14 us (3%)
  local copies, waits for them, and re-layouts  11.6 us (2%)
    psum x2, blocking collectives, tensor_total(): return lax.psum(value.astype(jnp.bfloat16), 'tensor').astype(jnp.float32)  245 us
    pallas_call x1, Pallas kernels, layer(): pl.pallas_call(layer_kernel, out_shape=(jax.ShapeDtypeStruct((rows, width...  97.4 us
    reduce_scatter x1, waiting for transfers between devices, body(): lax.psum_scatter(spread_out.astype(jnp.bfloat16), 'dp', scatter_dimension...  46.8 us
    all_gather x1, waiting for transfers between devices, body(): lax.all_gather(inner_correction_weights, 'dp', axis=0, tiled=True)  31.4 us
    reduce_scatter x1, waiting for transfers between devices, body(): lax.psum_scatter(spread_in.astype(jnp.bfloat16), 'dp', scatter_dimension=...  23 us
  transfers between devices with their start and end apart: 4, of which 3 were waited for; matrix products, arithmetic and copies ran while one was open for 3% of the time, Pallas kernels for 0%

profile of v1, /device:TPU:1, one launch (start us, length us, event | category | flops | bytes accessed | tf_op | source)
XLA Modules:
  0.0 488.4 jit_solution(18367810834292536486)
XLA Ops:
  7.2 0.0 all-gather.3.cloned.1.call-start
  7.2 0.7 all-gather.3.cloned.1.call-update
  7.9 0.0 all-gather.5.cloned.1.call-start
  7.9 0.7 all-gather.5.cloned.1.call-update
  8.6 0.0 reduce-scatter.3.cloned.1.call-start
  8.7 0.9 select_reduce_fusion
  9.5 0.0 copy-start.11
  9.6 0.5 copy-done.11
  10.1 0.7 fusion.8
  10.8 0.0 copy-start.9
  10.8 1.3 fusion.7
  12.1 31.4 %all-gather.3.cloned.1.call-done = bf16[64,64,256]{2,1,0:T(8,128)(2,1)} async-done(((bf16[16,64,256]{2,1,0:T(8,128)(2,1)}), bf16[64,64,256]{2,1,0:T(8,128)(2,1)}) %all-gather.3.cloned.1.call-update) | async-done | bytes 2097168 | tf_op jit(solution)/shard_map/all_gather | solution.py:449
  43.5 2.1 gather_fusion
  45.6 0.0 copy-start.2
  45.7 1.2 fusion
  46.8 123.3 %psum.14 = bf16[3,128,64]{1,2,0:T(8,128)(2,1)S(1)} all-reduce(bf16[3,128,64]{1,2,0:T(8,128)(2,1)S(1)} %fusion), channel_id=1, replica_groups=mesh['dp'=4,'tensor'=32] {'tensor'}, use_global_device_ids=true, to_apply=%region_1.2 | all-reduce | flops 24576 | bytes 98304 | tf_op jit(solution)/shard_map/psum | solution.py:423
  170.1 0.0 copy-done.2
  170.1 0.0 copy-start.4
  170.1 0.0 all-gather.5.cloned.1.call-done
  170.1 2.8 gather_fusion.1
  172.9 0.0 copy-start
  172.9 0.7 copy-done
  173.6 1.2 fusion.4
  174.8 0.0 copy-done.4
  174.8 0.0 copy-done.9
  174.8 97.4 %layer.1 = (bf16[384,256]{1,0:T(8,128)(2,1)}, f32[384,256]{1,0:T(8,128)}, bf16[384,448]{1,0:T(8,128)(2,1)}) custom-call(bf16[384,256]{1,0:T(8,128)(2,1)} %tokens_ref.1, bf16[384,256]{1,0:T(8,128)(2,1)} %cotangent_ref.1, bf16[448,8192]{1,0:T(8,128)(2,1)} %bitcast.27, bf16[448,8192]{1,0:T(8,128)(2,1)} %bitcast.28, bf16[448,8192]{1,0:T(8,128)(2,1)} %down_hbm.1, ...), custom_call_target="tpu_custom_call" | custom-call | tf_op jit(solution)/shard_map/layer/pallas_call | solution.py:382
  272.2 0.0 copy-start.1
  272.2 0.0 copy-start.5
  272.2 0.0 copy-start.10
  272.3 0.0 copy-start.12
  272.3 1.3 convolution_convert_fusion.3
  273.6 121.2 %psum.15 = bf16[3,128,64]{1,2,0:T(8,128)(2,1)S(1)} all-reduce(bf16[3,128,64]{1,2,0:T(8,128)(2,1)S(1)} %convolution_convert_fusion.3), channel_id=1, replica_groups=mesh['dp'=4,'tensor'=32] {'tensor'}, use_global_device_ids=true, to_apply=%region_2.3 | all-reduce | flops 24576 | bytes 98304 | tf_op jit(solution)/shard_map/psum | solution.py:423
  394.8 1.1 fusion.5
  395.9 3.9 convolution_convert_fusion.1
  399.8 0.0 reduce-scatter.3.cloned.1.call-update
  399.8 0.2 reduce-scatter.5.cloned.1.call-start
  400.1 0.0 copy-done.1
  400.1 0.0 copy-done.5
  400.1 0.0 copy-done.10
  400.1 0.2 convolution_multiply_fusion
  400.3 0.0 copy-done.12
  400.3 0.0 copy-start.3
  400.3 0.0 copy-start.8
  400.3 0.0 copy-start.6
  400.3 5.3 %convolution_convert_fusion = bf16[64,64,448]{2,0,1:T(8,128)(2,1)} fusion(f32[3,64,448]{2,1,0:T(8,128)S(1)} %convolution_multiply_fusion, s32[3]{0:T(128)S(1)} %copy-done.12), kind=kOutput, calls=%fused_computation.2 | convolution fusion | flops 67895488 | bytes 4014092 | tf_op jit(solution)/shard_map/bs,brf->srf/dot_general | solution.py:504
  405.6 0.0 copy-start.7
  405.6 0.0 reduce-scatter.5.cloned.1.call-update
  405.7 0.0 copy-done.3
  405.7 0.0 copy-done.8
  405.7 0.3 fusion.6
  405.9 0.0 copy-done.6
  405.9 0.7 fusion.2
  406.7 23.0 %reduce-scatter.3.cloned.1.call-done = bf16[16,64,256]{2,0,1:T(8,128)(2,1)} async-done(((bf16[64,64,256]{2,0,1:T(8,128)(2,1)}), bf16[16,64,256]{2,0,1:T(8,128)(2,1)}) %reduce-scatter.3.cloned.1.call-update) | async-done | bytes 524304 | tf_op jit(solution)/shard_map/reduce_scatter | solution.py:508
  429.6 2.0 copy.27
  431.6 46.8 %reduce-scatter.5.cloned.1.call-done = bf16[16,64,448]{2,0,1:T(8,128)(2,1)} async-done(((bf16[64,64,448]{2,0,1:T(8,128)(2,1)}), bf16[16,64,448]{2,0,1:T(8,128)(2,1)}) %reduce-scatter.5.cloned.1.call-update) | async-done | bytes 917520 | tf_op jit(solution)/shard_map/reduce_scatter | solution.py:511
  478.5 2.8 copy.28
  481.2 0.0 copy-done.7
  481.2 0.7 copy.37
  (2 shorter events, 0.0 us)
Async XLA Ops:
  7.2 36.3 %all-gather.3.cloned.1.call-start = ((), (), s32[]{:S(2)}) async-start(), calls=%async_computation.2 | async-start | bytes 2621440 | tf_op jit(solution)/shard_map/all_gather | solution.py:449
  7.9 162.2 %all-gather.5.cloned.1.call-start = ((), (), s32[]{:S(2)}) async-start(), calls=%async_computation.3 | async-start | bytes 5242880 | tf_op jit(solution)/shard_map/all_gather | solution.py:450
  8.6 421.0 %reduce-scatter.3.cloned.1.call-start = ((), (), s32[]{:S(2)}) async-start(), calls=%async_computation.4 | async-start | bytes 2621440 | tf_op jit(solution)/shard_map/reduce_scatter | solution.py:508
  9.5 0.5 copy-start.11
  10.8 164.0 %copy-start.9 = (f32[3,128]{1,0:T(4,128)}, f32[3,128]{1,0:T(4,128)S(1)}, u32[]{:S(2)}) copy-start(f32[3,128]{1,0:T(4,128)S(1)} %fusion.8) | copy-start | bytes 4612
  45.6 124.5 %copy-start.2 = (bf16[3,64,256]{2,1,0:T(8,128)(2,1)}, bf16[3,64,256]{2,1,0:T(8,128)(2,1)S(1)}, u32[]{:S(2)}) copy-start(bf16[3,64,256]{2,1,0:T(8,128)(2,1)S(1)} %gather_fusion) | copy-start | bytes 294916
  170.1 4.6 copy-start.4
  172.9 0.7 copy-start
  272.2 127.8 %copy-start.1 = (bf16[384,448]{1,0:T(8,128)(2,1)S(1)}, bf16[384,448]{1,0:T(8,128)(2,1)}, u32[]{:S(2)}) copy-start(bf16[384,448]{1,0:T(8,128)(2,1)} %get-tuple-element.9) | copy-start | bytes 1032196
  272.2 127.8 %copy-start.5 = (bf16[3,128,64]{1,2,0:T(8,128)(2,1)S(1)}, bf16[3,128,64]{1,2,0:T(8,128)(2,1)}, u32[]{:S(2)}) copy-start(bf16[3,128,64]{1,2,0:T(8,128)(2,1)} %copy-done.4) | copy-start | bytes 147460
  272.2 127.8 %copy-start.10 = (f32[3,128]{1,0:T(4,128)S(1)}, f32[3,128]{1,0:T(4,128)}, u32[]{:S(2)}) copy-start(f32[3,128]{1,0:T(4,128)} %copy-done.9) | copy-start | bytes 4612
  272.3 128.0 %copy-start.12 = (s32[3]{0:T(128)S(1)}, s32[3]{0:T(128)}, u32[]{:S(2)}) copy-start(s32[3]{0:T(128)} %copy-done.11) | copy-start | bytes 40
  399.8 78.6 %reduce-scatter.5.cloned.1.call-start = ((), (), s32[]{:S(2)}) async-start(), calls=%async_computation.5 | async-start | bytes 5242880 | tf_op jit(solution)/shard_map/reduce_scatter | solution.py:511
  400.3 5.4 %copy-start.3 = (bf16[3,64,256]{2,1,0:T(8,128)(2,1)S(1)}, bf16[3,64,256]{2,1,0:T(8,128)(2,1)}, u32[]{:S(2)}) copy-start(bf16[3,64,256]{2,1,0:T(8,128)(2,1)} %copy-done.2) | copy-start | bytes 294916
  400.3 5.4 %copy-start.8 = (f32[3,128]{1,0:T(4,128)S(1)}, f32[3,128]{1,0:T(4,128)}, u32[]{:S(2)}) copy-start(f32[3,128]{1,0:T(4,128)} %fusion.7) | copy-start | bytes 4612
  400.3 5.6 %copy-start.6 = (f32[384,256]{1,0:T(8,128)S(1)}, f32[384,256]{1,0:T(8,128)}, u32[]{:S(2)}) copy-start(f32[384,256]{1,0:T(8,128)} %get-tuple-element.8) | copy-start | bytes 1179652
  405.6 75.6 %copy-start.7 = (bf16[384,256]{1,0:T(8,128)(2,1)S(1)}, bf16[384,256]{1,0:T(8,128)(2,1)}, u32[]{:S(2)}) copy-start(bf16[384,256]{1,0:T(8,128)(2,1)} %get-tuple-element.26) | copy-start | bytes 589828
Sparse Core Ops, SparseCore 0:
  9.6 33.8 all-gather.2
  45.2 48.2 all-gather.4
  399.9 29.6 reduce-scatter.2
  431.9 46.5 reduce-scatter.4

commit v2 on v1

--- a/solution.py
+++ b/solution.py
@@ -1,5 +1,3 @@
-import functools
-
 import jax
 import jax.numpy as jnp
 from jax import lax
@@ -37,10 +35,16 @@
     gate_hbm,
     up_hbm,
     down_hbm,
-    extra_ref,
+    task_ref,
+    fill_ref,
+    slot_ref,
+    inner_hbm,
+    up_b_hbm,
     mixed_ref,
     item_ref,
-    d_up_ref,
+    grad_in_ref,
+    grad_out_ref,
+    place_ref,
     gathered,
     gate_w,
     up_w,
@@ -50,9 +54,28 @@
     dh_acc,
     hidden,
     d_gate,
-    to_partner,
+    d_up_ref,
     parts,
     landed,
+    own_tokens,
+    inner_own,
+    up_b_own,
+    task_land,
+    task_smem,
+    lent_in,
+    lent_out,
+    borrowed_in,
+    borrowed_out,
+    inner_rows,
+    up_rows,
+    partial,
+    sum_out,
+    sum_in,
+    low,
+    grads_in,
+    grads_out,
+    landed_in,
+    landed_out,
     own_sem,
     weight_sem,
     ag_send,
@@ -63,10 +86,21 @@
     half_recv,
     rs_send,
     rs_recv,
+    task_send,
+    task_recv,
+    lend_send,
+    lend_recv,
+    sum_send,
+    sum_recv,
+    grad_send,
+    grad_recv,
 ):
     rows, width = tokens_ref.shape
-    hidden_width = gate_acc.shape[1]
+    blocks = rows // BLOCK
     part_rows = rows // 2
+    to_partner = gathered.at[0]
+    y = lax.axis_index("dp")
+    owned_slots = inner_own.shape[0]
     me = lax.axis_index("tensor")
     core = lax.rem(me, 2)
     x = lax.rem(me // 2, SIDE)
@@ -95,14 +129,26 @@
         )
 
     barrier = pltpu.get_barrier_semaphore()
-    for peer in (partner, x_up, x_down, z_up, z_down):
+    x_far = index(z, lax.rem(x + 2, SIDE), core)
+    z_far = index(lax.rem(z + 2, SIDE), x, core)
+    for peer in (partner, x_up, x_down, z_up, z_down, x_far, z_far):
         pl.semaphore_signal(barrier, inc=1, device_id={"tensor": peer}, device_id_type=MESH)
+    for d in (1, 2, 3):
+        pl.semaphore_signal(barrier, inc=1, device_id={"dp": lax.rem(y + d, SIDE)}, device_id_type=MESH)
 
     own = [
         pltpu.make_async_copy(ref, gathered.at[a, me], own_sem.at[a])
         for a, ref in enumerate((tokens_ref, cotangent_ref))
     ]
     for copy in own:
+        copy.start()
+    locals_in = (
+        pltpu.make_async_copy(tokens_ref, own_tokens, own_sem.at[2]),
+        pltpu.make_async_copy(inner_hbm, inner_own, own_sem.at[3]),
+        pltpu.make_async_copy(up_b_hbm, up_b_own, own_sem.at[4]),
+        pltpu.make_async_copy(task_ref, task_smem.at[0], own_sem.at[5]),
+    )
+    for copy in locals_in:
         copy.start()
 
     def weight_copies(shard):
@@ -113,7 +159,23 @@
             pltpu.make_async_copy(down_hbm.at[:, pl.ds(at, width)], down_w.at[shard], weight_sem.at[2, shard]),
         )
 
-    pl.semaphore_wait(barrier, 5)
+    pl.semaphore_wait(barrier, 10)
+
+    def dp_remote(src, dst, send, recv, d):
+        return pltpu.make_async_remote_copy(
+            src_ref=src,
+            dst_ref=dst,
+            send_sem=send,
+            recv_sem=recv,
+            device_id={"dp": lax.rem(y + d, SIDE)},
+            device_id_type=MESH,
+        )
+
+    def task_copy(d):
+        return dp_remote(task_ref, task_land.at[d - 1], task_send.at[d - 1], task_recv.at[d - 1], d)
+
+    for d in (1, 2, 3):
+        task_copy(d).start()
 
     half = (slice(0, part_rows), slice(part_rows, rows))
 
@@ -165,7 +227,7 @@
     arrive(0, jnp.int32(0), True)
 
     def start_weights(kind):
-        def at_step(k, carry):
+        def one_step(k, carry):
             idx = pick(GATHER_ORDER, k)
             for shard in (mine(idx), theirs(idx)):
                 copies = weight_copies(shard)
@@ -173,7 +235,7 @@
                     copy.start()
             return carry
 
-        lax.fori_loop(0, CHIPS, at_step, 0)
+        lax.fori_loop(0, CHIPS, one_step, 0)
 
     start_weights(0)
     start_weights(1)
@@ -182,6 +244,119 @@
     dh_acc[...] = jnp.zeros_like(dh_acc)
 
     across = (((1,), (1,)), ((), ()))
+
+    def lend_copy(kind, d):
+        src, dst = ((lent_in, borrowed_in), (lent_out, borrowed_out))[kind]
+        return dp_remote(src.at[d], dst.at[d - 1], lend_send.at[kind, d - 1], lend_recv.at[kind, d - 1], d)
+
+    def spot_of(rank, j):
+        return slot_ref[task_smem[rank, 0, j]] - owned_slots * y
+
+    def lend():
+        for d in (1, 2, 3):
+            task_copy(d).wait_recv()
+        to_smem = pltpu.make_async_copy(task_land, task_smem.at[pl.ds(1, 3)], own_sem.at[6])
+        to_smem.start()
+        for copy in locals_in:
+            copy.wait()
+        to_smem.wait()
+        for kind, (own_ref, lent) in enumerate(((inner_own, lent_in), (up_b_own, lent_out))):
+            for d in (1, 2, 3, 0):
+                for j in range(blocks):
+                    spot = spot_of((SIDE - d) % SIDE, j)
+                    held = jnp.logical_and(spot >= 0, spot < owned_slots)
+                    safe = jnp.clip(spot, 0, owned_slots - 1)
+                    factor = jnp.where(held, 1.0, 0.0)
+                    lent[d, j] = (own_ref[safe].astype(jnp.float32) * factor).astype(jnp.bfloat16)
+                if d:
+                    lend_copy(kind, d).start()
+        for d in range(SIDE):
+            for j in range(blocks):
+                place_ref[d * blocks + j] = spot_of(d, j)
+
+    def borrow(kind):
+        lent, borrowed, held = ((lent_in, borrowed_in, inner_rows), (lent_out, borrowed_out, up_rows))[kind]
+        for d in (1, 2, 3):
+            lend_copy(kind, d).wait_recv()
+        held[...] = lent[0] + borrowed[0] + borrowed[1] + borrowed[2]
+
+    def block_at(b):
+        return slice(b * BLOCK, (b + 1) * BLOCK)
+
+    rank_half = partial.shape[0] // 2
+    here = pl.ds(pl.multiple_of(core * rank_half, rank_half), rank_half)
+    there = pl.ds(pl.multiple_of((1 - core) * rank_half, rank_half), rank_half)
+
+    def sum_copy(w, slot, src, to):
+        return remote(sum_out.at[w, src], sum_in.at[w, slot], sum_send.at[w, slot], sum_recv.at[w, slot], to)
+
+    def sum_pair(w):
+        for b in range(blocks):
+            if w == 0:
+                left, right = inner_rows[b], own_tokens[block_at(b), :]
+            else:
+                left, right = up_rows[b], d_up_ref[block_at(b), :]
+            partial[:, block_at(b)] = lax.dot_general(left, right, across, preferred_element_type=jnp.float32)
+        sum_out[w, 0] = partial[there, :].astype(jnp.bfloat16)
+        sum_copy(w, 0, 0, partner).start()
+
+    def sum_x(w):
+        sum_copy(w, 0, 0, partner).wait_recv()
+        sum_out[w, 1] = (partial[here, :] + sum_in[w, 0].astype(jnp.float32)).astype(jnp.bfloat16)
+        for d in (1, 2, 3):
+            sum_copy(w, d, 1, index(z, lax.rem(x + d, SIDE), core)).start()
+
+    def sum_four(w, own_slot, first):
+        total = sum_out[w, own_slot].astype(jnp.float32)
+        for d in range(3):
+            sum_copy(w, first + d, own_slot, partner).wait_recv()
+            total = total + sum_in[w, first + d].astype(jnp.float32)
+        return total.astype(jnp.bfloat16)
+
+    def sum_z(w):
+        sum_out[w, 2] = sum_four(w, 1, 1)
+        for d in (1, 2, 3):
+            sum_copy(w, 3 + d, 2, index(lax.rem(z + d, SIDE), x, core)).start()
+
+    def sum_back(w):
+        sum_out[w, 3] = sum_four(w, 2, 4)
+        sum_copy(w, 7, 3, partner).start()
+
+    def sum_end(w):
+        sum_copy(w, 7, 3, partner).wait_recv()
+        low[w, here, :] = sum_out[w, 3]
+        low[w, there, :] = sum_in[w, 7]
+        scale = (1.0, adapter_scale)[w]
+        for b in range(blocks):
+            live = lax.broadcasted_iota(jnp.int32, (2 * rank_half, BLOCK), 1) < fill_ref[b]
+            value = low[w, :, block_at(b)].astype(jnp.float32)
+            low[w, :, block_at(b)] = (scale * jnp.where(live, value, 0.0)).astype(jnp.bfloat16)
+
+    def grad_copy(kind, d):
+        src, dst = ((grads_in, landed_in), (grads_out, landed_out))[kind]
+        return dp_remote(src, dst.at[d - 1], grad_send.at[kind, d - 1], grad_recv.at[kind, d - 1], d)
+
+    def gradients(kind):
+        for b in range(blocks):
+            if kind == 0:
+                grads_in[b] = jnp.dot(
+                    low[1, :, block_at(b)], own_tokens[block_at(b), :], preferred_element_type=jnp.float32
+                ).astype(jnp.bfloat16)
+            else:
+                grads_out[b] = (
+                    adapter_scale
+                    * jnp.dot(low[0, :, block_at(b)], d_up_ref[block_at(b), :], preferred_element_type=jnp.float32)
+                ).astype(jnp.bfloat16)
+        for d in (1, 2, 3):
+            grad_copy(kind, d).start()
+
+    down_rank = (((0,), (0,)), ((), ()))
+
+    def adjoint():
+        for b in range(blocks):
+            gate_acc[block_at(b), 0:width] = lax.dot_general(
+                low[1, :, block_at(b)], inner_rows[b], down_rank, preferred_element_type=jnp.float32
+            )
 
     def use(a, shard):
         copies = weight_copies(shard)
@@ -214,11 +389,25 @@
                     pair_copy(a, shard, idx).wait_recv()
                 use(a, shard)
 
+    def at_step(k, step, do, *given):
+        @pl.when(k == step)
+        def _():
+            do(*given)
+
     def gather_step(k, carry):
         @pl.when(k == LAG)
         def _():
             arrive(1, jnp.int32(0), True)
 
+        at_step(k, 1, lend)
+        at_step(k, 5, borrow, 0)
+        at_step(k, 5, sum_pair, 0)
+        at_step(k, 7, sum_x, 0)
+        at_step(k, 10, sum_z, 0)
+        at_step(k, 14, sum_back, 0)
+        at_step(k, 17, sum_end, 0)
+        at_step(k, 18, borrow, 1)
+
         @pl.when(k < CHIPS + 1)
         def _():
             visit(0, k)
@@ -230,11 +419,16 @@
         return carry
 
     lax.fori_loop(0, CHIPS + 1 + LAG, gather_step, 0)
+
+    for b in range(blocks):
+        up_acc[block_at(b), :] += adapter_scale * lax.dot_general(
+            low[0, :, block_at(b)], up_rows[b], down_rank, preferred_element_type=jnp.float32
+        )
 
     def middle(block, carry):
         at = pl.ds(pl.multiple_of(block * 64, 64), 64)
         gate = gate_acc[at, :]
-        up = up_acc[at, :] + adapter_scale * extra_ref[at, :]
+        up = up_acc[at, :]
         d_hidden = dh_acc[at, :]
         sigmoid_gate = jax.nn.sigmoid(gate)
         activated = gate * sigmoid_gate
@@ -244,6 +438,19 @@
         return carry
 
     lax.fori_loop(0, rows // 64, middle, 0)
+    sum_pair(1)
+
+    def drain_tokens(k, carry):
+        pair_copy(0, me, k).wait_send()
+
+        @pl.when(k >= 1)
+        def _():
+            for h in (0, 1):
+                ag_copy(0, h, me, k, x_up).wait_send()
+
+        return carry
+
+    lax.fori_loop(0, CHIPS, drain_tokens, 0)
 
     def product(r, shard):
         if r == 0:
@@ -296,6 +503,8 @@
         total = parts[r, idx, half[h], :].astype(jnp.float32)
         for slot in slots:
             total = total + landed[r, h, slot].astype(jnp.float32)
+        if out is item_ref:
+            total = total + gate_acc[half[h], 0:width]
         if out is None:
             parts[r, idx, half[h], :] = total.astype(jnp.bfloat16)
         else:
@@ -322,6 +531,13 @@
 
     def mixed_step(k, carry):
         produce(0, k)
+        at_step(k, 1, gradients, 1)
+        at_step(k, 3, sum_x, 1)
+        at_step(k, 7, sum_z, 1)
+        at_step(k, 11, sum_back, 1)
+        at_step(k, 14, sum_end, 1)
+        at_step(k, 15, gradients, 0)
+        at_step(k, 16, adjoint)
         return carry
 
     lax.fori_loop(0, CHIPS + 2, mixed_step, 0)
@@ -350,14 +566,31 @@
         finish(1, 0, g)
         finish(1, 1, g)
 
+    grad_in_ref[0:blocks] = grads_in[...]
+    grad_out_ref[0:blocks] = grads_out[...]
+    for d in (1, 2, 3):
+        grad_copy(0, d).wait_recv()
+        grad_copy(1, d).wait_recv()
+        grad_in_ref[d * blocks : (d + 1) * blocks] = landed_in[d - 1]
+        grad_out_ref[d * blocks : (d + 1) * blocks] = landed_out[d - 1]
+    for d in (1, 2, 3):
+        task_copy(d).wait_send()
+        for kind in (0, 1):
+            lend_copy(kind, d).wait_send()
+            grad_copy(kind, d).wait_send()
+    for w in (0, 1):
+        for slot, src in enumerate((0, 1, 1, 1, 2, 2, 2, 3)):
+            sum_copy(w, slot, src, partner).wait_send()
+
     def drain(k, carry):
+        pair_copy(1, me, k).wait_send()
+
+        @pl.when(k >= 1)
+        def _():
+            for h in (0, 1):
+                ag_copy(1, h, me, k, x_up).wait_send()
+
         for a in (0, 1):
-            pair_copy(a, me, k).wait_send()
-
-            @pl.when(k >= 1)
-            def _():
-                for h in (0, 1):
-                    ag_copy(a, h, me, k, x_up).wait_send()
 
             @pl.when(k < 15)
             def _():
@@ -370,24 +603,32 @@
     lax.fori_loop(0, CHIPS, drain, 0)
 
 
-def layer(tokens, cotangent, gate_weight, up_weight, down_weight, extra):
+def layer(
+    tokens, cotangent, gate_weight, up_weight, down_weight, block_task, block_fill, task_slot, inner, up_b
+):
     rows, width = tokens.shape
     hidden_width = gate_weight.shape[1]
     shards = gate_weight.shape[0] // width
     half = rows // 2
+    blocks = rows // BLOCK
+    owned, rank, _ = inner.shape
     any_spec = pl.BlockSpec(memory_space=pl.ANY)
     vmem_spec = pl.BlockSpec(memory_space=pltpu.VMEM)
+    smem_spec = pl.BlockSpec(memory_space=pltpu.SMEM)
     bf16, f32 = jnp.bfloat16, jnp.float32
     dma = pltpu.SemaphoreType.DMA
+    tasks = jnp.broadcast_to(jnp.pad(block_task, (0, 128 - blocks))[None, :], (8, 128))
     return pl.pallas_call(
         layer_kernel,
         out_shape=(
             jax.ShapeDtypeStruct((rows, width), bf16),
-            jax.ShapeDtypeStruct((rows, width), f32),
-            jax.ShapeDtypeStruct((rows, hidden_width), bf16),
+            jax.ShapeDtypeStruct((rows, width), bf16),
+            jax.ShapeDtypeStruct((SIDE * blocks, rank, width), bf16),
+            jax.ShapeDtypeStruct((SIDE * blocks, rank, hidden_width), bf16),
+            jax.ShapeDtypeStruct((SIDE * blocks,), jnp.int32),
         ),
-        in_specs=[any_spec] * 5 + [vmem_spec],
-        out_specs=(vmem_spec,) * 3,
+        in_specs=[any_spec] * 5 + [vmem_spec, smem_spec, smem_spec, any_spec, any_spec],
+        out_specs=(vmem_spec,) * 4 + (smem_spec,),
         scratch_shapes=[
             pltpu.VMEM((2, shards, rows, width), bf16),
             pltpu.VMEM((shards, hidden_width, width), bf16),
@@ -398,10 +639,29 @@
             pltpu.VMEM((rows, hidden_width), f32),
             pltpu.VMEM((rows, hidden_width), bf16),
             pltpu.VMEM((rows, hidden_width), bf16),
-            pltpu.VMEM((CHIPS, rows, width), bf16),
+            pltpu.VMEM((rows, hidden_width), bf16),
             pltpu.VMEM((2, CHIPS, rows, width), bf16),
             pltpu.VMEM((2, 2, 15, half, width), bf16),
-            dma((2,)),
+            pltpu.VMEM((rows, width), bf16),
+            pltpu.VMEM((owned, rank, width), bf16),
+            pltpu.VMEM((owned, rank, hidden_width), bf16),
+            pltpu.VMEM((3, 8, 128), jnp.int32),
+            pltpu.SMEM((SIDE, 8, 128), jnp.int32),
+            pltpu.VMEM((SIDE, blocks, rank, width), bf16),
+            pltpu.VMEM((SIDE, blocks, rank, hidden_width), bf16),
+            pltpu.VMEM((3, blocks, rank, width), bf16),
+            pltpu.VMEM((3, blocks, rank, hidden_width), bf16),
+            pltpu.VMEM((blocks, rank, width), bf16),
+            pltpu.VMEM((blocks, rank, hidden_width), bf16),
+            pltpu.VMEM((rank, rows), f32),
+            pltpu.VMEM((2, 4, rank // 2, rows), bf16),
+            pltpu.VMEM((2, 8, rank // 2, rows), bf16),
+            pltpu.VMEM((2, rank, rows), bf16),
+            pltpu.VMEM((blocks, rank, width), bf16),
+            pltpu.VMEM((blocks, rank, hidden_width), bf16),
+            pltpu.VMEM((3, blocks, rank, width), bf16),
+            pltpu.VMEM((3, blocks, rank, hidden_width), bf16),
+            dma((7,)),
             dma((3, shards)),
             dma((2, 2, CHIPS)),
             dma((2, 2, CHIPS)),
@@ -411,16 +671,63 @@
             dma((2, CHIPS)),
             dma((2, 2, 15)),
             dma((2, 2, 15)),
+            dma((3,)),
+            dma((3,)),
+            dma((2, 3)),
+            dma((2, 3)),
+            dma((2, 8)),
+            dma((2, 8)),
+            dma((2, 3)),
+            dma((2, 3)),
         ],
         compiler_params=pltpu.CompilerParams(
             collective_id=0, has_side_effects=True, vmem_limit_bytes=67043328
         ),
         name="layer",
-    )(tokens, cotangent, gate_weight.T, up_weight.T, down_weight, extra)
-
-
-def tensor_total(value):
-    return lax.psum(value.astype(jnp.bfloat16), "tensor").astype(jnp.float32)
+    )(
+        tokens,
+        cotangent,
+        gate_weight.T,
+        up_weight.T,
+        down_weight,
+        tasks,
+        block_fill,
+        task_slot,
+        inner,
+        up_b,
+    )
+
+
+def spread_kernel(place_ref, mixed_in, item_in, grads_in, grads_out, mixed, item, owned_in, owned_out, sum_in, sum_out):
+    mixed[...] = mixed_in[...]
+    item[...] = item_in[...]
+    for grads, total, owned in ((grads_in, sum_in, owned_in), (grads_out, sum_out, owned_out)):
+        total[...] = jnp.zeros_like(total)
+
+        @pl.loop(0, grads.shape[0])
+        def _(b):
+            spot = place_ref[b]
+
+            @pl.when(jnp.logical_and(spot >= 0, spot < total.shape[0]))
+            def _():
+                total[spot] += grads[b].astype(jnp.float32)
+
+        owned[...] = total[...].astype(jnp.bfloat16)
+
+
+def spread(place, mixed, item, grads_in, grads_out, owned):
+    vmem_spec = pl.BlockSpec(memory_space=pltpu.VMEM)
+    shapes = [(owned,) + g.shape[1:] for g in (grads_in, grads_out)]
+    return pl.pallas_call(
+        spread_kernel,
+        out_shape=tuple(
+            jax.ShapeDtypeStruct(s, jnp.bfloat16) for s in (mixed.shape, item.shape, *shapes)
+        ),
+        in_specs=[pl.BlockSpec(memory_space=pltpu.SMEM)] + [vmem_spec] * 4,
+        out_specs=(vmem_spec,) * 4,
+        scratch_shapes=[pltpu.VMEM(s, jnp.float32) for s in shapes],
+        name="spread",
+    )(place, mixed, item, grads_in, grads_out)
 
 
 def body(
@@ -435,84 +742,19 @@
     inner_correction_weights,
     up_b,
 ):
-    row_count, local_width = tokens.shape
-    block_count = block_task.shape[0]
-    hidden_width = gate_weight.shape[1]
-    task_ids = jnp.arange(task_slot.shape[0], dtype=jnp.int32)
-    segment_owner_index = jnp.sum(
-        jnp.where(block_task[:, None] == task_ids[None, :], task_slot[None, :], 0), axis=1
+    mixed, item, grads_in, grads_out, place = layer(
+        tokens,
+        cotangent,
+        gate_weight,
+        up_weight,
+        down_weight,
+        block_task,
+        block_fill,
+        task_slot,
+        inner_correction_weights,
+        up_b,
     )
-    enabled_flags = (jnp.arange(BLOCK, dtype=jnp.int32)[None, :] < block_fill[:, None]).astype(
-        jnp.float32
-    )[..., None]
-    complete_arrivals, every_out = (
-        lax.all_gather(inner_correction_weights, "dp", axis=0, tiled=True),
-        lax.all_gather(up_b, "dp", axis=0, tiled=True),
-    )
-    correction_source_vector = complete_arrivals[segment_owner_index]
-    up_factor_output = every_out[segment_owner_index]
-    portion_clusters = tokens.reshape(block_count, BLOCK, local_width)
-    narrow_product = (
-        tensor_total(
-            jnp.einsum(
-                "imk,iok->imo",
-                portion_clusters,
-                correction_source_vector,
-                preferred_element_type=jnp.float32,
-            )
-        )
-        * enabled_flags
-    )
-    low_rank_b_output = narrow_product.astype(jnp.bfloat16)
-    adapter_up_output = jnp.einsum(
-        "vam,vmk->vak", low_rank_b_output, up_factor_output, preferred_element_type=jnp.float32
-    ).reshape(row_count, hidden_width)
-    mixed, fixed, d_up = layer(tokens, cotangent, gate_weight, up_weight, down_weight, adapter_up_output)
-    gradient_per_block = d_up.reshape(block_count, BLOCK, hidden_width)
-    narrow_derivative = (
-        adapter_scale
-        * tensor_total(
-            jnp.einsum(
-                "oge,oce->ogc",
-                gradient_per_block,
-                up_factor_output,
-                preferred_element_type=jnp.float32,
-            )
-        )
-        * enabled_flags
-    )
-    exterior_multiplier_dual = narrow_derivative.astype(jnp.bfloat16)
-    adjoint_of_correction = jnp.einsum(
-        "lxu,luz->lxz",
-        exterior_multiplier_dual,
-        correction_source_vector,
-        preferred_element_type=jnp.float32,
-    ).reshape(row_count, local_width)
-    item_derivative = (fixed + adjoint_of_correction).astype(jnp.bfloat16)
-    arriving_slope = jnp.einsum(
-        "bqf,bqm->bfm",
-        exterior_multiplier_dual,
-        portion_clusters,
-        preferred_element_type=jnp.float32,
-    )
-    output_gradient = adapter_scale * jnp.einsum(
-        "wvd,wvg->wdg", low_rank_b_output, gradient_per_block, preferred_element_type=jnp.float32
-    )
-    slot_ids = jnp.arange(task_slot.shape[0], dtype=jnp.int32)
-    one_hot = (segment_owner_index[:, None] == slot_ids[None, :]).astype(jnp.float32)
-    spread_in = jnp.einsum("bs,brd->srd", one_hot, arriving_slope, precision=lax.Precision.HIGHEST)
-    spread_out = jnp.einsum(
-        "bs,brf->srf", one_hot, output_gradient, precision=lax.Precision.HIGHEST
-    )
-    owned_in, owned_out = (
-        lax.psum_scatter(
-            spread_in.astype(jnp.bfloat16), "dp", scatter_dimension=0, tiled=True
-        ).astype(jnp.float32),
-        lax.psum_scatter(
-            spread_out.astype(jnp.bfloat16), "dp", scatter_dimension=0, tiled=True
-        ).astype(jnp.float32),
-    )
-    return (mixed, item_derivative, owned_in.astype(jnp.bfloat16), owned_out.astype(jnp.bfloat16))
+    return spread(place, mixed, item, grads_in, grads_out, up_b.shape[0])
 
 
 def solution(mesh):

time: 489 us -> 116 us (0.24)
  blocking collectives: 245 us -> 0 us
  waiting for transfers between devices: 103 us -> 0 us
  Pallas kernels: 97.4 us -> 112 us
  matrix products: 14.4 us -> 0 us
  between operations: 14 us -> 0.64 us
  local copies, waits for them, and re-layouts: 11.6 us -> 1.26 us
    psum x2 -> x0, blocking collectives: 245 us -> none  [tensor_total(): return lax.psum(value.astype(jnp.bfloat16), 'tensor').astype(jnp.float32)]
    reduce_scatter x2 -> x0, waiting for transfers between devices: 69.8 us -> none  [the longest x1 46.8 us: body(): lax.psum_scatter(spread_out.astype(jnp.bfloat16), 'dp', scatter_dimension...]
    all_gather x2 -> x0, waiting for transfers between devices: 31.4 us -> none  [the longest x1 31.4 us: body(): lax.all_gather(inner_correction_weights, 'dp', axis=0, tiled=True)]
    dot_general x8 -> x0, matrix products: 14.4 us -> none  [the longest x1 5.29 us: body(): jnp.einsum('bs,brf->srf', one_hot, output_gradient, precision=lax.Precisi...]
    pallas_call x1, Pallas kernels: 97.4 us -> 108 us  [layer(): pl.pallas_call(layer_kernel, out_shape=(jax.ShapeDtypeStruct((rows, width...]
    unnamed x29 -> x0, local copies, waits for them, and re-layouts: 6.67 us -> none
    gather x2 -> x0, local copies, waits for them, and re-layouts: 4.91 us -> none  [the longest x1 2.76 us: body(): up_factor_output = every_out[segment_owner_index]]
  transfers between devices with their start and end apart: 4 -> 0, of which waited for: 3 -> 0; matrix products, arithmetic and copies ran while one was open for 3% -> 0% of each run, Pallas kernels for 0% -> 0%
where the time goes in v2:
time: 116 us; the launch traced here: 114 us
  Pallas kernels  112 us (97%)
  local copies, waits for them, and re-layouts  1.26 us (1%)
    pallas_call x1, Pallas kernels, layer(): pl.pallas_call(layer_kernel, out_shape=(jax.ShapeDtypeStruct((rows, width...  108 us
    pallas_call x1, Pallas kernels, spread(): pl.pallas_call(spread_kernel, out_shape=tuple((jax.ShapeDtypeStruct(s, jn...  3.4 us

profile of v2, /device:TPU:1, one launch (start us, length us, event | category | flops | bytes accessed | tf_op | source)
XLA Modules:
  0.0 113.7 jit_solution(11337347268914879352)
XLA Ops:
  0.6 0.7 pad.4
  1.3 0.6 broadcast_in_dim.2.task_ref
  1.9 108.4 %layer.1 = (bf16[384,256]{1,0:T(8,128)(2,1)}, bf16[384,256]{1,0:T(8,128)(2,1)}, bf16[12,64,256]{2,1,0:T(8,128)(2,1)}, bf16[12,64,448]{2,1,0:T(8,128)(2,1)}, s32[12]{0:T(128)}) custom-call(bf16[384,256]{1,0:T(8,128)(2,1)} %tokens_ref.1, bf16[384,256]{1,0:T(8,128)(2,1)} %cotangent_ref.1, bf16[448,8192]{1,0:T(8,128)(2,1)} %bitcast.2, ...), custom_call_target="tpu_custom_call" | custom-call | tf_op jit(solution)/shard_map/layer/pallas_call | solution.py:621
  110.3 3.4 %spread.1 = (bf16[384,256]{1,0:T(8,128)(2,1)}, bf16[384,256]{1,0:T(8,128)(2,1)}, bf16[16,64,256]{2,1,0:T(8,128)(2,1)}, bf16[16,64,448]{2,1,0:T(8,128)(2,1)}) custom-call(s32[12]{0:T(128)} %get-tuple-element.9.place_ref, bf16[384,256]{1,0:T(8,128)(2,1)} %get-tuple-element.10.mixed_in, bf16[384,256]{1,0:T(8,128)(2,1)} %get-tuple-element.11.item_in, ...), custom_call_target="tpu_custom_call" | custom-call | tf_op jit(solution)/shard_map/spread/pallas_call | solution.py:721

commit v3 on v2

v3 whole, which is shorter than its diff:
```python
import functools

import jax
import jax.numpy as jnp
from jax import lax
from jax.experimental import pallas as pl
from jax.experimental.pallas import tpu as pltpu
from jax.sharding import PartitionSpec as P

BLOCK = 128
SIDE = 4
CHIPS = SIDE * SIDE
MESH = pl.DeviceIdType.MESH
COT_SEND = 5
COT = 6
LEND = 0
LOW = 5
HIDE = 18
MIX = 18
ITEM = 24
BEHIND = 3
COMBINE = ((19, 17, 16, 14), (17, 15, 14, 11))
FINISH = ((22, 21, 20, 18), (19, 18, 17, 14))

GATHER_ORDER = (0, 4, 1, 8, 2, 12, 3, 5, 6, 10, 9, 13, 7, 14, 11, 15)
SCATTER_ORDER = (15, 14, 11, 13, 7, 12, 3, 10, 9, 5, 6, 8, 2, 4, 1, 0)

adapter_scale = 0.25


def packed(values, bits):
    word = sum(v << (bits * n) for n, v in enumerate(values))
    return jnp.int32(word - (1 << 32) if word >= 1 << 31 else word)


def pick(table, step):
    word = jnp.where(step < 8, packed(table[:8], 4), packed(table[8:], 4))
    return (word >> (4 * (step & 7))) & 15


def shifted(position, offset, sign):
    deltas = jnp.where(sign > 0, packed((0, 3, 1, 2), 2), packed((0, 1, 3, 2), 2))
    return (position + (deltas >> (2 * offset))) & 3


def timed(k, events):
    if not events:
        return
    steps = [e[0] for e in events]
    if steps[0] == steps[-1]:

        @pl.when(k == steps[0])
        def _():
            for _, do in events:
                do()

        return
    middle = steps[len(steps) // 2]
    if middle == steps[0]:
        middle = next(n for n in steps if n > middle)

    @pl.when(k < middle)
    def _():
        timed(k, [e for e in events if e[0] < middle])

    @pl.when(k >= middle)
    def _():
        timed(k, [e for e in events if e[0] >= middle])


def layer_kernel(
    tokens_ref,
    cotangent_ref,
    gate_hbm,
    up_hbm,
    down_hbm,
    task_ref,
    fill_ref,
    slot_ref,
    inner_hbm,
    up_b_hbm,
    mixed_ref,
    item_ref,
    grad_in_ref,
    grad_out_ref,
    place_ref,
    gathered,
    gate_up_w,
    down_w,
    gate_up,
    slope,
    dh_acc,
    hidden,
    d_both,
    d_up_ref,
    made,
    parts,
    landed,
    own_tokens,
    inner_own,
    up_b_own,
    task_tile,
    task_land,
    task_smem,
    lent_in,
    lent_out,
    borrowed_in,
    borrowed_out,
    inner_rows,
    up_rows,
    partial,
    sum_out,
    sum_in,
    low,
    grads_in,
    grads_out,
    landed_in,
    landed_out,
    own_sem,
    weight_sem,
    ag_send,
    ag_recv,
    pair_send,
    pair_recv,
    half_send,
    half_recv,
    rs_send,
    rs_recv,
    task_send,
    task_recv,
    lend_send,
    lend_recv,
    sum_send,
    sum_recv,
    grad_send,
    grad_recv,
    out_sem,
):
    rows, width = tokens_ref.shape
    blocks = rows // BLOCK
    part_rows = rows // 2
    hidden_width = hidden.shape[1]
    y = lax.axis_index("dp")
    owned_slots = inner_own.shape[0]
    me = lax.axis_index("tensor")
    core = me & 1
    x = (me >> 1) & 3
    z = me >> 3
    sign = 1 - 2 * core
    partner = me + sign

    here_columns = pl.ds(pl.multiple_of(core * width, width), width)
    there_columns = pl.ds(pl.multiple_of((1 - core) * width, width), width)
    my_chip = me >> 1

    def index(zz, xx, cc):
        return (zz * SIDE + xx) * 2 + cc

    x_up = index(z, (x + sign + SIDE) & 3, core)
    x_down = index(z, (x - sign + SIDE) & 3, core)
    z_up = index((z + sign + SIDE) & 3, x, core)
    z_down = index((z - sign + SIDE) & 3, x, core)
    along = {"x": (x_up, x_down), "z": (z_up, z_down)}

    def mine(idx):
        return shifted(z, idx & 3, sign) * SIDE + shifted(x, idx >> 2, sign)

    def theirs(idx):
        return shifted(z, idx & 3, -sign) * SIDE + shifted(x, idx >> 2, -sign)

    def remote(src, dst, send, recv, to):
        return pltpu.make_async_remote_copy(
            src_ref=src, dst_ref=dst, send_sem=send, recv_sem=recv, device_id={"tensor": to}, device_id_type=MESH
        )

    barrier = pltpu.get_barrier_semaphore()
    x_far = index(z, (x + 2) & 3, core)
    z_far = index((z + 2) & 3, x, core)
    for peer in (partner, x_up, x_down, z_up, z_down, x_far, z_far):
        pl.semaphore_signal(barrier, inc=1, device_id={"tensor": peer}, device_id_type=MESH)
    for d in (1, 2, 3):
        pl.semaphore_signal(barrier, inc=1, device_id={"dp": (y + d) & 3}, device_id_type=MESH)

    own = [
        pltpu.make_async_copy(ref, gathered.at[a, my_chip, :, here_columns], own_sem.at[a])
        for a, ref in enumerate((tokens_ref, cotangent_ref))
    ]
    for copy in own:
        copy.start()
    locals_in = (
        pltpu.make_async_copy(tokens_ref, own_tokens, own_sem.at[2]),
        pltpu.make_async_copy(inner_hbm, inner_own, own_sem.at[3]),
        pltpu.make_async_copy(up_b_hbm, up_b_own, own_sem.at[4]),
    )
    for copy in locals_in:
        copy.start()

    gate_part, up_part = slice(0, hidden_width), slice(hidden_width, 2 * hidden_width)

    def weight_copies(chip):
        at = pl.ds(pl.multiple_of(chip * 2 * width, 2 * width), 2 * width)
        return (
            pltpu.make_async_copy(gate_hbm.at[:, at], gate_up_w.at[chip, gate_part, :], weight_sem.at[0, chip]),
            pltpu.make_async_copy(up_hbm.at[:, at], gate_up_w.at[chip, up_part, :], weight_sem.at[1, chip]),
            pltpu.make_async_copy(down_hbm.at[:, at], down_w.at[chip], weight_sem.at[2, chip]),
        )

    lanes = lax.broadcasted_iota(jnp.int32, task_tile.shape, 1)
    tile = jnp.zeros(task_tile.shape, jnp.int32)
    for j in range(blocks):
        tile = jnp.where(lanes == j, task_ref[j], tile)
    task_tile[...] = tile

    pl.semaphore_wait(barrier, 10)

    def dp_remote(src, dst, send, recv, d):
        return pltpu.make_async_remote_copy(
            src_ref=src,
            dst_ref=dst,
            send_sem=send,
            recv_sem=recv,
            device_id={"dp": (y + d) & 3},
            device_id_type=MESH,
        )

    def task_copy(d):
        return dp_remote(task_tile, task_land.at[d - 1], task_send.at[d - 1], task_recv.at[d - 1], d)

    for d in (1, 2, 3):
        task_copy(d).start()

    half = (slice(0, part_rows), slice(part_rows, rows))

    def ag_copy(a, h, chip, idx, to):
        ref = gathered.at[a, chip, half[h], here_columns]
        return remote(ref, ref, ag_send.at[a, h, idx], ag_recv.at[a, h, idx], to)

    def arrive(a, idx, first):
        ox, oz = idx >> 2, idx & 3
        chip = mine(idx)
        if first:
            own[a].wait()
        for h, (name_f, name_g) in enumerate((("x", "z"), ("z", "x"))):
            of, og = (ox, oz) if h == 0 else (oz, ox)

            def spot(f, g, h=h):
                return f * SIDE + g if h == 0 else g * SIDE + f

            if not first:
                ag_copy(a, h, chip, idx, x_up).wait_recv()
            f_up, f_down = along[name_f]
            g_up, g_down = along[name_g]
            if first:
                ag_copy(a, h, chip, spot(1, 0), f_up).start()
                ag_copy(a, h, chip, spot(2, 0), f_down).start()
                ag_copy(a, h, chip, spot(0, 1), g_up).start()
                ag_copy(a, h, chip, spot(0, 2), g_down).start()
            else:

                @pl.when(jnp.logical_and(og == 0, of == 1))
                def _():
                    ag_copy(a, h, chip, spot(3, 0), f_up).start()

                @pl.when(og == 0)
                def _():
                    ag_copy(a, h, chip, spot(of, 1), g_up).start()
                    ag_copy(a, h, chip, spot(of, 2), g_down).start()

                @pl.when(og == 1)
                def _():
                    ag_copy(a, h, chip, spot(of, 3), g_up).start()

        pair_copy(a, chip, idx, here_columns).start()

    def pair_copy(a, chip, idx, columns):
        ref = gathered.at[a, chip, :, columns]
        return remote(ref, ref, pair_send.at[a, idx], pair_recv.at[a, idx], partner)

    arrive(0, jnp.int32(0), True)

    def start_weights(k, carry):
        for copy in weight_copies(mine(pick(GATHER_ORDER, k))):
            copy.start()
        return carry

    lax.fori_loop(0, CHIPS, start_weights, 0)
    gate_up[...] = jnp.zeros_like(gate_up)
    dh_acc[...] = jnp.zeros_like(dh_acc)

    across = (((1,), (1,)), ((), ()))

    def lend_copy(kind, d):
        src, dst = ((lent_in, borrowed_in), (lent_out, borrowed_out))[kind]
        return dp_remote(src.at[d], dst.at[d - 1], lend_send.at[kind, d - 1], lend_recv.at[kind, d - 1], d)

    def spot_of(rank, j):
        task = task_smem[rank - 1, 0, j] if rank else task_ref[j]
        return slot_ref[task] - owned_slots * y

    def lend():
        for d in (1, 2, 3):
            task_copy(d).wait_recv()
        to_smem = pltpu.make_async_copy(task_land, task_smem, own_sem.at[5])
        to_smem.start()
        for copy in locals_in:
            copy.wait()
        to_smem.wait()
        for kind, (own_ref, lent) in enumerate(((inner_own, lent_in), (up_b_own, lent_out))):
            for d in (1, 2, 3, 0):
                for j in range(blocks):
                    spot = spot_of((SIDE - d) % SIDE, j)
                    held = jnp.logical_and(spot >= 0, spot < owned_slots)
                    safe = jnp.clip(spot, 0, owned_slots - 1)
                    factor = jnp.where(held, 1.0, 0.0)
                    lent[d, j] = (own_ref[safe].astype(jnp.float32) * factor).astype(jnp.bfloat16)
                if d:
                    lend_copy(kind, d).start()
        for d in range(SIDE):
            for j in range(blocks):
                place_ref[d * blocks + j] = spot_of(d, j)

    def borrow(kind):
        lent, borrowed, held = ((lent_in, borrowed_in, inner_rows), (lent_out, borrowed_out, up_rows))[kind]
        for d in (1, 2, 3):
            lend_copy(kind, d).wait_recv()
        held[...] = lent[0] + borrowed[0] + borrowed[1] + borrowed[2]

    def block_at(b):
        return slice(b * BLOCK, (b + 1) * BLOCK)

    rank_half = partial.shape[0] // 2
    here = pl.ds(pl.multiple_of(core * rank_half, rank_half), rank_half)
    there = pl.ds(pl.multiple_of((1 - core) * rank_half, rank_half), rank_half)

    def sum_copy(w, slot, src, to):
        return remote(sum_out.at[w, src], sum_in.at[w, slot], sum_send.at[w, slot], sum_recv.at[w, slot], to)

    def sum_pair(w):
        for b in range(blocks):
            if w == 0:
                left, right = inner_rows[b], own_tokens[block_at(b), :]
            else:
                left, right = up_rows[b], d_up_ref[block_at(b), :]
            partial[:, block_at(b)] = lax.dot_general(left, right, across, preferred_element_type=jnp.float32)
        sum_out[w, 0] = partial[there, :].astype(jnp.bfloat16)
        sum_copy(w, 0, 0, partner).start()

    def sum_x(w):
        sum_copy(w, 0, 0, partner).wait_recv()
        sum_out[w, 1] = (partial[here, :] + sum_in[w, 0].astype(jnp.float32)).astype(jnp.bfloat16)
        for d in (1, 2, 3):
            sum_copy(w, d, 1, index(z, (x + d) & 3, core)).start()

    def sum_four(w, own_slot, first):
        total = sum_out[w, own_slot].astype(jnp.float32)
        for d in range(3):
            sum_copy(w, first + d, own_slot, partner).wait_recv()
            total = total + sum_in[w, first + d].astype(jnp.float32)
        return total.astype(jnp.bfloat16)

    def sum_z(w):
        sum_out[w, 2] = sum_four(w, 1, 1)
        for d in (1, 2, 3):
            sum_copy(w, 3 + d, 2, index((z + d) & 3, x, core)).start()

    def sum_back(w):
        sum_out[w, 3] = sum_four(w, 2, 4)
        sum_copy(w, 7, 3, partner).start()

    def sum_end(w):
        sum_copy(w, 7, 3, partner).wait_recv()
        low[w, here, :] = sum_out[w, 3]
        low[w, there, :] = sum_in[w, 7]
        scale = (1.0, adapter_scale)[w]
        for b in range(blocks):
            live = lax.broadcasted_iota(jnp.int32, (2 * rank_half, BLOCK), 1) < fill_ref[b]
            value = low[w, :, block_at(b)].astype(jnp.float32)
            low[w, :, block_at(b)] = (scale * jnp.where(live, value, 0.0)).astype(jnp.bfloat16)

    def grad_copy(kind, d):
        src, dst = ((grads_in, landed_in), (grads_out, landed_out))[kind]
        return dp_remote(src, dst.at[d - 1], grad_send.at[kind, d - 1], grad_recv.at[kind, d - 1], d)

    def gradients(kind):
        for b in range(blocks):
            if kind == 0:
                grads_in[b] = jnp.dot(
                    low[1, :, block_at(b)], own_tokens[block_at(b), :], preferred_element_type=jnp.float32
                ).astype(jnp.bfloat16)
            else:
                grads_out[b] = (
                    adapter_scale
                    * jnp.dot(low[0, :, block_at(b)], d_up_ref[block_at(b), :], preferred_element_type=jnp.float32)
                ).astype(jnp.bfloat16)
        for d in (1, 2, 3):
            grad_copy(kind, d).start()
        out_copy(kind, 0).start()

    def out_copy(kind, d):
        ref, own_grads, landed_grads = ((grad_in_ref, grads_in, landed_in), (grad_out_ref, grads_out, landed_out))[kind]
        src = landed_grads.at[d - 1] if d else own_grads
        return pltpu.make_async_copy(src, ref.at[pl.ds(d * blocks, blocks)], out_sem.at[kind, d])

    def collect():
        for kind in (1, 0):
            for d in (1, 2, 3):
                grad_copy(kind, d).wait_recv()
                out_copy(kind, d).start()

    down_rank = (((0,), (0,)), ((), ()))

    def adjoint():
        for b in range(blocks):
            gate_up[block_at(b), 0:width] = lax.dot_general(
                low[1, :, block_at(b)], inner_rows[b], down_rank, preferred_element_type=jnp.float32
            )

    def use(a, chip):
        if a == 0:
            for copy in weight_copies(chip):
                copy.wait()
        total, weights = ((gate_up, gate_up_w), (dh_acc, down_w))[a]
        total[...] += lax.dot_general(
            gathered[a, chip], weights[chip], across, preferred_element_type=jnp.float32
        )

    def visit(a, k):
        @pl.when(jnp.logical_and(k >= 1, k < CHIPS))
        def _():
            arrive(a, pick(GATHER_ORDER, k), False)

        @pl.when(jnp.logical_and(k >= 1, k < CHIPS + 1))
        def _():
            idx = pick(GATHER_ORDER, k - 1)
            pair_copy(a, theirs(idx), idx, there_columns).wait_recv()

        @pl.when(k >= BEHIND)
        def _():
            use(a, mine(pick(GATHER_ORDER, k - BEHIND)))

    def hide():
        for b in range(blocks):
            slope[block_at(b), :] = adapter_scale * lax.dot_general(
                low[0, :, block_at(b)], up_rows[b], down_rank, preferred_element_type=jnp.float32
            )

        def some_rows(n, carry):
            at = pl.ds(pl.multiple_of(n * 64, 64), 64)
            gate = gate_up[at, gate_part]
            up = gate_up[at, up_part] + slope[at, :]
            sigmoid_gate = jax.nn.sigmoid(gate)
            activated = gate * sigmoid_gate
            hidden[at, :] = (activated * up).astype(jnp.bfloat16)
            gate_up[at, gate_part] = activated
            slope[at, :] = up * sigmoid_gate * (1.0 + gate * (1.0 - sigmoid_gate))
            return carry

        lax.fori_loop(0, rows // 64, some_rows, 0)

    def differentiate():
        def some_rows(n, carry):
            at = pl.ds(pl.multiple_of(n * 64, 64), 64)
            d_hidden = dh_acc[at, :]
            d_up = (d_hidden * gate_up[at, gate_part]).astype(jnp.bfloat16)
            d_both[at, gate_part] = (d_hidden * slope[at, :]).astype(jnp.bfloat16)
            d_both[at, up_part] = d_up
            d_up_ref[at, :] = d_up
            return carry

        lax.fori_loop(0, rows // 64, some_rows, 0)

    def product(r, chip):
        left, right = ((hidden, down_w), (d_both, gate_up_w))[r]
        return jnp.dot(left[...], right[chip], preferred_element_type=jnp.float32).astype(jnp.bfloat16)

    def mirrored(idx):
        swap = packed((0, 2, 1, 3), 2)
        return ((swap >> (2 * (idx >> 2))) & 3) * SIDE + ((swap >> (2 * (idx & 3))) & 3)

    def half_copy(r, slot, idx):
        to = mirrored(idx)
        return remote(
            made.at[r, slot, :, there_columns], parts.at[r, to], half_send.at[r, idx], half_recv.at[r, to], partner
        )

    def half_landed(r, idx):
        return remote(
            made.at[r, 0, :, there_columns], parts.at[r, idx], half_send.at[r, idx], half_recv.at[r, idx], partner
        )

    def rs_copy(r, h, idx, slot, to):
        return remote(parts.at[r, idx, half[h], :], landed.at[r, h, slot], rs_send.at[r, h, slot], rs_recv.at[r, h, slot], to)

    names = (("z", "x"), ("x", "z"))

    def place(h, f, g):
        return g * SIDE + f if h == 0 else f * SIDE + g

    def produce(r, k):
        @pl.when(k < CHIPS)
        def _():
            idx = pick(SCATTER_ORDER, k)
            slot = k & 3

            @pl.when(k >= 4)
            def _():
                half_copy(r, slot, pick(SCATTER_ORDER, k - 4)).wait_send()

            made[r, slot] = product(r, mine(idx))
            half_copy(r, slot, idx).start()

        @pl.when(k >= BEHIND)
        def _():
            idx = pick(SCATTER_ORDER, k - BEHIND)
            half_landed(r, idx).wait_recv()
            own_part = made[r, (k - BEHIND) & 3, :, here_columns].astype(jnp.float32)
            parts[r, idx] = (own_part + parts[r, idx].astype(jnp.float32)).astype(jnp.bfloat16)
            ox, oz = idx >> 2, idx & 3
            for h in (0, 1):
                of, og = (oz, ox) if h == 0 else (ox, oz)
                f_up, f_down = along[names[h][0]]

                @pl.when(of == 3)
                def _():
                    rs_copy(r, h, idx, og, f_down).start()

                @pl.when(of == 2)
                def _():
                    rs_copy(r, h, idx, SIDE + og, f_up).start()

    def add_in(r, h, idx, slots, out=None):
        for slot in slots:
            rs_copy(r, h, idx, slot, x_up).wait_recv()
        total = parts[r, idx, half[h], :].astype(jnp.float32)
        for slot in slots:
            total = total + landed[r, h, slot].astype(jnp.float32)
        if out is item_ref:
            total = total + gate_up[half[h], 0:width]
        if out is None:
            parts[r, idx, half[h], :] = total.astype(jnp.bfloat16)
        else:
            out[half[h], :] = total.astype(out.dtype)

    def combine(r, h, g):
        idx = place(h, 1, g)
        add_in(r, h, idx, (g,))
        rs_copy(r, h, idx, 2 * SIDE + g, along[names[h][0]][1]).start()

    def finish(r, h, g):
        idx = place(h, 0, g)
        add_in(r, h, idx, (SIDE + g, 2 * SIDE + g))
        g_up, g_down = along[names[h][1]]
        if g == 3:
            rs_copy(r, h, idx, 3 * SIDE, g_down).start()
        elif g == 2:
            rs_copy(r, h, idx, 3 * SIDE + 1, g_up).start()
        elif g == 1:
            add_in(r, h, idx, (3 * SIDE,))
            rs_copy(r, h, idx, 3 * SIDE + 2, g_down).start()
        else:
            add_in(r, h, idx, (3 * SIDE + 1, 3 * SIDE + 2), (mixed_ref, item_ref)[r])

    def both_halves(do, r, g):
        do(r, 0, g)
        do(r, 1, g)

    early = [
        (COT_SEND, lambda: arrive(1, jnp.int32(0), True)),
        (LEND, lend),
        (LOW, lambda: borrow(0)),
        (LOW, lambda: sum_pair(0)),
        (LOW + 2, lambda: sum_x(0)),
        (LOW + 5, lambda: sum_z(0)),
        (LOW + 8, lambda: sum_back(0)),
        (HIDE, lambda: borrow(1)),
        (HIDE, lambda: sum_end(0)),
        (HIDE, hide),
        (ITEM, differentiate),
        (ITEM + 1, lambda: sum_pair(1)),
        (ITEM + 1, lambda: gradients(1)),
        (ITEM + 3, lambda: sum_x(1)),
        (ITEM + 6, lambda: sum_z(1)),
        (ITEM + 9, lambda: sum_back(1)),
        (ITEM + 12, lambda: sum_end(1)),
        (ITEM + 12, lambda: gradients(0)),
        (ITEM + 13, adjoint),
        (ITEM + FINISH[1][1], collect),
    ]
    late = []
    for r, start in ((0, MIX), (1, ITEM)):
        for g in (3, 2, 1, 0):
            late.append((start + COMBINE[r][g], functools.partial(both_halves, combine, r, g)))
            late.append((start + FINISH[r][g], functools.partial(both_halves, finish, r, g)))
    early.sort(key=lambda e: e[0])
    late.sort(key=lambda e: e[0])

    def step(k, carry):
        @pl.when(k < COT + CHIPS + BEHIND)
        def _():
            for a, start in ((0, 0), (1, COT)):

                @pl.when(jnp.logical_and(k >= start, k < start + CHIPS + BEHIND))
                def _():
                    visit(a, k - start)

        timed(k, early)

        @pl.when(k >= MIX)
        def _():
            for r, start in ((0, MIX), (1, ITEM)):

                @pl.when(jnp.logical_and(k >= start, k < start + CHIPS + BEHIND))
                def _():
                    produce(r, k - start)

            timed(k, late)

        return carry

    lax.fori_loop(0, ITEM + FINISH[1][0] + 1, step, 0)
    for d in (1, 2, 3):
        task_copy(d).wait_send()
        for kind in (0, 1):
            lend_copy(kind, d).wait_send()
            grad_copy(kind, d).wait_send()
    for w in (0, 1):
        for slot, src in enumerate((0, 1, 1, 1, 2, 2, 2, 3)):
            sum_copy(w, slot, src, partner).wait_send()

    for kind in (0, 1):
        for d in range(SIDE):
            out_copy(kind, d).wait()
    for r in (0, 1):
        for k in range(CHIPS - 4, CHIPS):
            half_landed(r, SCATTER_ORDER[k]).wait_send()

    def drain(k, carry):
        for a in (0, 1):
            pair_copy(a, my_chip, k, here_columns).wait_send()

            @pl.when(k >= 1)
            def _():
                for h in (0, 1):
                    ag_copy(a, h, my_chip, k, x_up).wait_send()

            @pl.when(k < 15)
            def _():
                for h in (0, 1):
                    rs_copy(a, h, k, k, x_up).wait_send()

        return carry

    lax.fori_loop(0, CHIPS, drain, 0)


def layer(
    tokens, cotangent, gate_weight, up_weight, down_weight, block_task, block_fill, task_slot, inner, up_b
):
    rows, width = tokens.shape
    hidden_width = gate_weight.shape[1]
    half = rows // 2
    blocks = rows // BLOCK
    owned, rank, _ = inner.shape
    any_spec = pl.BlockSpec(memory_space=pl.ANY)
    vmem_spec = pl.BlockSpec(memory_space=pltpu.VMEM)
    smem_spec = pl.BlockSpec(memory_space=pltpu.SMEM)
    bf16, f32 = jnp.bfloat16, jnp.float32
    dma = pltpu.SemaphoreType.DMA
    return pl.pallas_call(
        layer_kernel,
        out_shape=(
            jax.ShapeDtypeStruct((rows, width), bf16),
            jax.ShapeDtypeStruct((rows, width), bf16),
            jax.ShapeDtypeStruct((SIDE * blocks, rank, width), bf16),
            jax.ShapeDtypeStruct((SIDE * blocks, rank, hidden_width), bf16),
            jax.ShapeDtypeStruct((SIDE * blocks,), jnp.int32),
        ),
        in_specs=[any_spec] * 5 + [smem_spec] * 3 + [any_spec] * 2,
        out_specs=(vmem_spec, vmem_spec, any_spec, any_spec, smem_spec),
        scratch_shapes=[
            pltpu.VMEM((2, CHIPS, rows, 2 * width), bf16),
            pltpu.VMEM((CHIPS, 2 * hidden_width, 2 * width), bf16),
            pltpu.VMEM((CHIPS, hidden_width, 2 * width), bf16),
            pltpu.VMEM((rows, 2 * hidden_width), f32),
            pltpu.VMEM((rows, hidden_width), f32),
            pltpu.VMEM((rows, hidden_width), f32),
            pltpu.VMEM((rows, hidden_width), bf16),
            pltpu.VMEM((rows, 2 * hidden_width), bf16),
            pltpu.VMEM((rows, hidden_width), bf16),
            pltpu.VMEM((2, 4, rows, 2 * width), bf16),
            pltpu.VMEM((2, CHIPS, rows, width), bf16),
            pltpu.VMEM((2, 2, 15, half, width), bf16),
            pltpu.VMEM((rows, width), bf16),
            pltpu.VMEM((owned, rank, width), bf16),
            pltpu.VMEM((owned, rank, hidden_width), bf16),
            pltpu.VMEM((8, 128), jnp.int32),
            pltpu.VMEM((3, 8, 128), jnp.int32),
            pltpu.SMEM((3, 8, 128), jnp.int32),
            pltpu.VMEM((SIDE, blocks, rank, width), bf16),
            pltpu.VMEM((SIDE, blocks, rank, hidden_width), bf16),
            pltpu.VMEM((3, blocks, rank, width), bf16),
            pltpu.VMEM((3, blocks, rank, hidden_width), bf16),
            pltpu.VMEM((blocks, rank, width), bf16),
            pltpu.VMEM((blocks, rank, hidden_width), bf16),
            pltpu.VMEM((rank, rows), f32),
            pltpu.VMEM((2, 4, rank // 2, rows), bf16),
            pltpu.VMEM((2, 8, rank // 2, rows), bf16),
            pltpu.VMEM((2, rank, rows), bf16),
            pltpu.VMEM((blocks, rank, width), bf16),
            pltpu.VMEM((blocks, rank, hidden_width), bf16),
            pltpu.VMEM((3, blocks, rank, width), bf16),
            pltpu.VMEM((3, blocks, rank, hidden_width), bf16),
            dma((6,)),
            dma((3, CHIPS)),
            dma((2, 2, CHIPS)),
            dma((2, 2, CHIPS)),
            dma((2, CHIPS)),
            dma((2, CHIPS)),
            dma((2, CHIPS)),
            dma((2, CHIPS)),
            dma((2, 2, 15)),
            dma((2, 2, 15)),
            dma((3,)),
            dma((3,)),
            dma((2, 3)),
            dma((2, 3)),
            dma((2, 8)),
            dma((2, 8)),
            dma((2, 3)),
            dma((2, 3)),
            dma((2, SIDE)),
        ],
        compiler_params=pltpu.CompilerParams(
            collective_id=0, has_side_effects=True, vmem_limit_bytes=67043328
        ),
        name="layer",
    )(
        tokens,
        cotangent,
        gate_weight.T,
        up_weight.T,
        down_weight,
        block_task,
        block_fill,
        task_slot,
        inner,
        up_b,
    )


def spread_kernel(place_ref, mixed_in, item_in, grads_in, grads_out, mixed, item, owned_in, owned_out, sum_in, sum_out):
    mixed[...] = mixed_in[...]
    item[...] = item_in[...]
    for grads, total, owned in ((grads_in, sum_in, owned_in), (grads_out, sum_out, owned_out)):
        total[...] = jnp.zeros_like(total)

        @pl.loop(0, grads.shape[0])
        def _(b):
            spot = place_ref[b]

            @pl.when(jnp.logical_and(spot >= 0, spot < total.shape[0]))
            def _():
                total[spot] += grads[b].astype(jnp.float32)

        owned[...] = total[...].astype(jnp.bfloat16)


def spread(place, mixed, item, grads_in, grads_out, owned):
    vmem_spec = pl.BlockSpec(memory_space=pltpu.VMEM)
    shapes = [(owned,) + g.shape[1:] for g in (grads_in, grads_out)]
    return pl.pallas_call(
        spread_kernel,
        out_shape=tuple(
            jax.ShapeDtypeStruct(s, jnp.bfloat16) for s in (mixed.shape, item.shape, *shapes)
        ),
        in_specs=[pl.BlockSpec(memory_space=pltpu.SMEM)] + [vmem_spec] * 4,
        out_specs=(vmem_spec,) * 4,
        scratch_shapes=[pltpu.VMEM(s, jnp.float32) for s in shapes],
        name="spread",
    )(place, mixed, item, grads_in, grads_out)


def body(
    tokens,
    cotangent,
    gate_weight,
    up_weight,
    down_weight,
    block_task,
    block_fill,
    task_slot,
    inner_correction_weights,
    up_b,
):
    mixed, item, grads_in, grads_out, place = layer(
        tokens,
        cotangent,
        gate_weight,
        up_weight,
        down_weight,
        block_task,
        block_fill,
        task_slot,
        inner_correction_weights,
        up_b,
    )
    return spread(place, mixed, item, grads_in, grads_out, up_b.shape[0])


def solution(mesh):
    return jax.shard_map(
        body,
        mesh=mesh,
        in_specs=(
            P("dp", "tensor"),
            P("dp", "tensor"),
            P(None, "tensor"),
            P(None, "tensor"),
            P("tensor", None),
            P("dp"),
            P("dp"),
            P(),
            P("dp", None, "tensor"),
            P("dp", None, "tensor"),
        ),
        out_specs=(
            P("dp", "tensor"),
            P("dp", "tensor"),
            P("dp", None, "tensor"),
            P("dp", None, "tensor"),
        ),
        check_vma=False,
    )
```

time: 116 us -> 102 us (0.88); the launches traced: 114 us -> 102 us
  Pallas kernels: 112 us -> 101 us
  local copies, waits for them, and re-layouts: 1.26 us -> 0 us
    pallas_call x1, Pallas kernels: 108 us -> 97.6 us  [layer(): pl.pallas_call(layer_kernel, out_shape=(jax.ShapeDtypeStruct((rows, width...]
where the time goes in v3:
time: 102 us
  Pallas kernels  101 us (99%)
    pallas_call x1, Pallas kernels, layer(): pl.pallas_call(layer_kernel, out_shape=(jax.ShapeDtypeStruct((rows, width...  97.6 us
    pallas_call x1, Pallas kernels, spread(): pl.pallas_call(spread_kernel, out_shape=tuple((jax.ShapeDtypeStruct(s, jn...  3.44 us

profile of v3, /device:TPU:1, one launch (start us, length us, event | category | flops | bytes accessed | tf_op | source)
XLA Modules:
  0.0 101.7 jit_solution(15409484432291045120)
XLA Ops:
  0.6 97.6 %layer.1 = (bf16[384,256]{1,0:T(8,128)(2,1)}, bf16[384,256]{1,0:T(8,128)(2,1)}, bf16[12,64,256]{2,1,0:T(8,128)(2,1)}, bf16[12,64,448]{2,1,0:T(8,128)(2,1)}, s32[12]{0:T(128)}) custom-call(bf16[384,256]{1,0:T(8,128)(2,1)} %tokens_ref.1, bf16[384,256]{1,0:T(8,128)(2,1)} %cotangent_ref.1, bf16[448,8192]{1,0:T(8,128)(2,1)} %bitcast.2, ...), custom_call_target="tpu_custom_call" | custom-call | tf_op jit(solution)/shard_map/layer/pallas_call | solution.py:669
  98.3 3.4 %spread.1 = (bf16[384,256]{1,0:T(8,128)(2,1)}, bf16[384,256]{1,0:T(8,128)(2,1)}, bf16[16,64,256]{2,1,0:T(8,128)(2,1)}, bf16[16,64,448]{2,1,0:T(8,128)(2,1)}) custom-call(s32[12]{0:T(128)} %get-tuple-element.9.place_ref, bf16[384,256]{1,0:T(8,128)(2,1)} %get-tuple-element.10.mixed_in, bf16[384,256]{1,0:T(8,128)(2,1)} %get-tuple-element.11.item_in, ...), custom_call_target="tpu_custom_call" | custom-call | tf_op jit(solution)/shard_map/spread/pallas_call | solution.py:771

commit v4 on v3

--- a/solution.py
+++ b/solution.py
@@ -11,19 +11,19 @@
 SIDE = 4
 CHIPS = SIDE * SIDE
 MESH = pl.DeviceIdType.MESH
-COT_SEND = 5
-COT = 6
+COT = 1
 LEND = 0
-LOW = 5
+LOW = 9
 HIDE = 18
 MIX = 18
-ITEM = 24
+ITEM = 19
 BEHIND = 3
-COMBINE = ((19, 17, 16, 14), (17, 15, 14, 11))
-FINISH = ((22, 21, 20, 18), (19, 18, 17, 14))
+SCATTER_BEHIND = 2
+COMBINE = ((18, 15, 14, 11), (17, 15, 14, 13))
+FINISH = ((21, 20, 19, 16), (20, 19, 18, 16))
 
 GATHER_ORDER = (0, 4, 1, 8, 2, 12, 3, 5, 6, 10, 9, 13, 7, 14, 11, 15)
-SCATTER_ORDER = (15, 14, 11, 13, 7, 12, 3, 10, 9, 5, 6, 8, 2, 4, 1, 0)
+SCATTER_ORDER = (15, 12, 3, 14, 13, 11, 7, 10, 5, 9, 6, 8, 4, 2, 1, 0)
 
 adapter_scale = 0.25
 
@@ -277,6 +277,7 @@
         return remote(ref, ref, pair_send.at[a, idx], pair_recv.at[a, idx], partner)
 
     arrive(0, jnp.int32(0), True)
+    arrive(1, jnp.int32(0), True)
 
     def start_weights(k, carry):
         for copy in weight_copies(mine(pick(GATHER_ORDER, k))):
@@ -509,11 +510,11 @@
             made[r, slot] = product(r, mine(idx))
             half_copy(r, slot, idx).start()
 
-        @pl.when(k >= BEHIND)
+        @pl.when(k >= SCATTER_BEHIND)
         def _():
-            idx = pick(SCATTER_ORDER, k - BEHIND)
+            idx = pick(SCATTER_ORDER, k - SCATTER_BEHIND)
             half_landed(r, idx).wait_recv()
-            own_part = made[r, (k - BEHIND) & 3, :, here_columns].astype(jnp.float32)
+            own_part = made[r, (k - SCATTER_BEHIND) & 3, :, here_columns].astype(jnp.float32)
             parts[r, idx] = (own_part + parts[r, idx].astype(jnp.float32)).astype(jnp.bfloat16)
             ox, oz = idx >> 2, idx & 3
             for h in (0, 1):
@@ -564,8 +565,40 @@
         do(r, 0, g)
         do(r, 1, g)
 
+    def drain():
+        for d in (1, 2, 3):
+            task_copy(d).wait_send()
+            for kind in (0, 1):
+                lend_copy(kind, d).wait_send()
+                grad_copy(kind, d).wait_send()
+        for w in (0, 1):
+            for slot, src in enumerate((0, 1, 1, 1, 2, 2, 2, 3)):
+                sum_copy(w, slot, src, partner).wait_send()
+        for kind in (0, 1):
+            for d in range(SIDE):
+                out_copy(kind, d).wait()
+        for k in range(CHIPS - 4, CHIPS):
+            half_landed(0, SCATTER_ORDER[k]).wait_send()
+
+        def one(k, carry):
+            for a in (0, 1):
+                pair_copy(a, my_chip, k, here_columns).wait_send()
+
+                @pl.when(k >= 1)
+                def _():
+                    for h in (0, 1):
+                        ag_copy(a, h, my_chip, k, x_up).wait_send()
+
+            @pl.when(k < 15)
+            def _():
+                for h in (0, 1):
+                    rs_copy(0, h, 0, k, x_up).wait_send()
+
+            return carry
+
+        lax.fori_loop(0, CHIPS, one, 0)
+
     early = [
-        (COT_SEND, lambda: arrive(1, jnp.int32(0), True)),
         (LEND, lend),
         (LOW, lambda: borrow(0)),
         (LOW, lambda: sum_pair(0)),
@@ -585,6 +618,7 @@
         (ITEM + 12, lambda: gradients(0)),
         (ITEM + 13, adjoint),
         (ITEM + FINISH[1][1], collect),
+        (ITEM + FINISH[1][0], drain),
     ]
     late = []
     for r, start in ((0, MIX), (1, ITEM)):
@@ -609,7 +643,7 @@
         def _():
             for r, start in ((0, MIX), (1, ITEM)):
 
-                @pl.when(jnp.logical_and(k >= start, k < start + CHIPS + BEHIND))
+                @pl.when(jnp.logical_and(k >= start, k < start + CHIPS + SCATTER_BEHIND))
                 def _():
                     produce(r, k - start)
 
@@ -617,40 +651,12 @@
 
         return carry
 
-    lax.fori_loop(0, ITEM + FINISH[1][0] + 1, step, 0)
-    for d in (1, 2, 3):
-        task_copy(d).wait_send()
-        for kind in (0, 1):
-            lend_copy(kind, d).wait_send()
-            grad_copy(kind, d).wait_send()
-    for w in (0, 1):
-        for slot, src in enumerate((0, 1, 1, 1, 2, 2, 2, 3)):
-            sum_copy(w, slot, src, partner).wait_send()
-
-    for kind in (0, 1):
-        for d in range(SIDE):
-            out_copy(kind, d).wait()
-    for r in (0, 1):
-        for k in range(CHIPS - 4, CHIPS):
-            half_landed(r, SCATTER_ORDER[k]).wait_send()
-
-    def drain(k, carry):
-        for a in (0, 1):
-            pair_copy(a, my_chip, k, here_columns).wait_send()
-
-            @pl.when(k >= 1)
-            def _():
-                for h in (0, 1):
-                    ag_copy(a, h, my_chip, k, x_up).wait_send()
-
-            @pl.when(k < 15)
-            def _():
-                for h in (0, 1):
-                    rs_copy(a, h, k, k, x_up).wait_send()
-
-        return carry
-
-    lax.fori_loop(0, CHIPS, drain, 0)
+    lax.fori_loop(0, max(MIX + FINISH[0][0], ITEM + FINISH[1][0]) + 1, step, 0)
+    for k in range(CHIPS - 4, CHIPS):
+        half_landed(1, SCATTER_ORDER[k]).wait_send()
+    for h in (0, 1):
+        for slot in range(15):
+            rs_copy(1, h, 0, slot, x_up).wait_send()
 
 
 def layer(

time: 102 us -> 99.1 us (0.972)
  Pallas kernels: 101 us -> 98.3 us
    pallas_call x1, Pallas kernels: 97.6 us -> 94.9 us  [layer(): pl.pallas_call(layer_kernel, out_shape=(jax.ShapeDtypeStruct((rows, width...]
where the time goes in v4:
time: 99.1 us; the launch traced here: 98.9 us
  Pallas kernels  98.3 us (99%)
    pallas_call x1, Pallas kernels, layer(): pl.pallas_call(layer_kernel, out_shape=(jax.ShapeDtypeStruct((rows, width...  94.9 us
    pallas_call x1, Pallas kernels, spread(): pl.pallas_call(spread_kernel, out_shape=tuple((jax.ShapeDtypeStruct(s, jn...  3.4 us

profile of v4, /device:TPU:1, one launch (start us, length us, event | category | flops | bytes accessed | tf_op | source)
XLA Modules:
  0.0 98.9 jit_solution(14178066055217930103)
XLA Ops:
  0.6 94.9 %layer.1 = (bf16[384,256]{1,0:T(8,128)(2,1)}, bf16[384,256]{1,0:T(8,128)(2,1)}, bf16[12,64,256]{2,1,0:T(8,128)(2,1)}, bf16[12,64,448]{2,1,0:T(8,128)(2,1)}, s32[12]{0:T(128)}) custom-call(bf16[384,256]{1,0:T(8,128)(2,1)} %tokens_ref.1, bf16[384,256]{1,0:T(8,128)(2,1)} %cotangent_ref.1, bf16[448,8192]{1,0:T(8,128)(2,1)} %bitcast.2, ...), custom_call_target="tpu_custom_call" | custom-call | tf_op jit(solution)/shard_map/layer/pallas_call | solution.py:675
  95.5 3.4 %spread.1 = (bf16[384,256]{1,0:T(8,128)(2,1)}, bf16[384,256]{1,0:T(8,128)(2,1)}, bf16[16,64,256]{2,1,0:T(8,128)(2,1)}, bf16[16,64,448]{2,1,0:T(8,128)(2,1)}) custom-call(s32[12]{0:T(128)} %get-tuple-element.9.place_ref, bf16[384,256]{1,0:T(8,128)(2,1)} %get-tuple-element.10.mixed_in, bf16[384,256]{1,0:T(8,128)(2,1)} %get-tuple-element.11.item_in, ...), custom_call_target="tpu_custom_call" | custom-call | tf_op jit(solution)/shard_map/spread/pallas_call | solution.py:777

commit v5 on v4

--- a/solution.py
+++ b/solution.py
@@ -19,8 +19,8 @@
 ITEM = 19
 BEHIND = 3
 SCATTER_BEHIND = 2
-COMBINE = ((18, 15, 14, 11), (17, 15, 14, 13))
-FINISH = ((21, 20, 19, 16), (20, 19, 18, 16))
+COMBINE = ((18, 14, 13, 9), (17, 15, 14, 13))
+FINISH = ((21, 20, 18, 14), (20, 19, 18, 16))
 
 GATHER_ORDER = (0, 4, 1, 8, 2, 12, 3, 5, 6, 10, 9, 13, 7, 14, 11, 15)
 SCATTER_ORDER = (15, 12, 3, 14, 13, 11, 7, 10, 5, 9, 6, 8, 4, 2, 1, 0)

time: 99.1 us -> 98.8 us (level)
  no operation moved by 1% of the time
where the time goes in v5:
time: 98.8 us; the launch traced here: 98.7 us
  Pallas kernels  98 us (99%)
    pallas_call x1, Pallas kernels, layer(): pl.pallas_call(layer_kernel, out_shape=(jax.ShapeDtypeStruct((rows, width...  94.6 us
    pallas_call x1, Pallas kernels, spread(): pl.pallas_call(spread_kernel, out_shape=tuple((jax.ShapeDtypeStruct(s, jn...  3.41 us

profile of v5, /device:TPU:1, one launch (start us, length us, event | category | flops | bytes accessed | tf_op | source)
XLA Modules:
  0.0 98.7 jit_solution(8021685166982116704)
XLA Ops:
  0.6 94.6 %layer.1 = (bf16[384,256]{1,0:T(8,128)(2,1)}, bf16[384,256]{1,0:T(8,128)(2,1)}, bf16[12,64,256]{2,1,0:T(8,128)(2,1)}, bf16[12,64,448]{2,1,0:T(8,128)(2,1)}, s32[12]{0:T(128)}) custom-call(bf16[384,256]{1,0:T(8,128)(2,1)} %tokens_ref.1, bf16[384,256]{1,0:T(8,128)(2,1)} %cotangent_ref.1, bf16[448,8192]{1,0:T(8,128)(2,1)} %bitcast.2, ...), custom_call_target="tpu_custom_call" | custom-call | tf_op jit(solution)/shard_map/layer/pallas_call | solution.py:675
  95.2 3.4 %spread.1 = (bf16[384,256]{1,0:T(8,128)(2,1)}, bf16[384,256]{1,0:T(8,128)(2,1)}, bf16[16,64,256]{2,1,0:T(8,128)(2,1)}, bf16[16,64,448]{2,1,0:T(8,128)(2,1)}) custom-call(s32[12]{0:T(128)} %get-tuple-element.9.place_ref, bf16[384,256]{1,0:T(8,128)(2,1)} %get-tuple-element.10.mixed_in, bf16[384,256]{1,0:T(8,128)(2,1)} %get-tuple-element.11.item_in, ...), custom_call_target="tpu_custom_call" | custom-call | tf_op jit(solution)/shard_map/spread/pallas_call | solution.py:777
